TPU v7x, 32 devices: a whole 2x2x4 slice. The times are simulated.
32 devices in a mesh: grp: 2 (over x), tm: 16 (over z, y, core).
Axes of the slice: x: 2, y: 2, z: 4, core: 2. Of those that a mesh axis runs over, the one named last changes fastest.
Arguments:
- features: bfloat16 [128, 16, 4608], P(('grp', 'tm')), parts along dimension 0, may hold values from -6 to 6
- gains: float32 [4, 192], replicated, may hold values from 0.1 to 1.9
- conv_weights: bfloat16 [4, 3, 3, 3, 192, 192], replicated, may hold values from -0.078125 to 0.078125
- video_frames: int32 [8], P('grp'), parts along dimension 0, may hold values from 1 to 48, as said below
- video_start: int32 [8], P('grp'), parts along dimension 0, may hold values from 0 to 15, as said below
Outputs:
- decoded: bfloat16 [128, 16, 4608], P(('grp', 'tm')), parts along dimension 0
There are 2 independent parts, one for each index of `grp`. A program takes and returns all parts, laid end to end along the dimension named above; an argument that names none is the same for every part. Nothing has to cross between parts.
Inputs may be any that keep to these rules, and one draw needn't show every extreme that they name: video_start[0] = 0 and the starts rise strictly; video v takes the spans from video_start[v] up to the next video's start (16 for the last), and the videos fill all spans. `video_frames`: video v has its number of spans times 4 frames, less 0 to 3 empty slots at the end of its last span; the last video has 2 spans and 3 empty slots; one other video has 12 spans and no empty slot; the rest have one span each.
All inputs are finite; a program needn't handle non-finite values.
Results may differ from a plain program's by a relative error of at most 0.0056.
Values may be sent and summed in bfloat16 or wider, within the bound.
No kernel may reach another device: no remote copies, remote signals or barrier semaphores. Data moves between devices by JAX's collectives and lax.ppermute only.
A program may use at most 64 MiB of HBM per device.

v0:
```python
import functools

import jax
import jax.numpy as jnp
from jax import lax
from jax.experimental import pallas as pl
from jax.experimental.pallas import tpu as pltpu
from jax.sharding import PartitionSpec as P

LANES = 128
HALO = 2
STEP = 4
VMEM = pltpu.VMEM


def passed_along(value, axis):
    count = lax.axis_size(axis)
    return lax.ppermute(value, axis, [(i, i + 1) for i in range(count - 1)])


def low_half(shape):
    return lax.broadcasted_iota(jnp.int32, shape, len(shape) - 1) < LANES // 2


def swap_half(value):
    return pltpu.roll(value, LANES // 2, axis=value.ndim - 1)


def activate(main, rest, gain_main, gain_rest, channels):
    total = jnp.sum(main * main + rest * rest, axis=-1, keepdims=True)
    inverse = lax.rsqrt(total * (1.0 / channels) + 1e-06)

    def silu(value, gain):
        scaled = value * inverse * gain
        half = 0.5 * scaled
        return half * jnp.tanh(half) + half

    return silu(main, gain_main), silu(rest, gain_rest)


def load_gain(gains, gain_pad, index):
    return gain_pad[index, 0][None, None, :], gain_pad[index, 1][None, None, :]


def fill_gain(gains, gain_pad):
    count, channels = gains.shape
    gain_pad[...] = jnp.zeros_like(gain_pad)
    for k in range(count):
        gain_pad[k, 0:1, :] = gains[k : k + 1, 0:LANES]
        gain_pad[k, 1:2, 0 : channels - LANES] = gains[k : k + 1, LANES:channels]


def unpack_dense(source, frame, chunk):
    rows = source.shape[1]
    width = STEP * 192
    block = source[frame, :, pl.ds(pl.multiple_of(chunk * width, LANES), width)].astype(jnp.float32)
    tile = [block[:, LANES * i : LANES * (i + 1)] for i in range(width // LANES)]
    low = low_half((rows, LANES))
    main, rest = [], []
    for i in range(0, len(tile), 3):
        rolled_b, rolled_c = swap_half(tile[i + 1]), swap_half(tile[i + 2])
        main += [tile[i], jnp.where(low, rolled_b, rolled_c)]
        rest += [jnp.where(low, tile[i + 1], 0.0), jnp.where(low, rolled_c, 0.0)]
    return jnp.stack(main), jnp.stack(rest)


def pack_dense(target, frame, chunk, main, rest):
    rows = target.shape[1]
    width = STEP * 192
    low = low_half((rows, LANES))
    tile = []
    for i in range(0, STEP, 2):
        rolled = swap_half(main[i + 1])
        tile += [main[i], jnp.where(low, rest[i], rolled), jnp.where(low, rolled, swap_half(rest[i + 1]))]
    block = jnp.concatenate(tile, axis=-1).astype(target.dtype)
    target[frame, :, pl.ds(pl.multiple_of(chunk * width, LANES), width)] = block


def unpack_wire(source, frame, chunk, keep):
    cols = source.shape[1] * 2 // 3
    main = source[frame, pl.ds(STEP * chunk, STEP)].astype(jnp.float32)
    pair = source[frame, pl.ds(cols + STEP // 2 * chunk, STEP // 2)].astype(jnp.float32)
    low = low_half(pair.shape)
    rest = jnp.stack([jnp.where(low, pair, 0.0), jnp.where(low, swap_half(pair), 0.0)], axis=1)
    return main * keep, rest.reshape(main.shape) * keep


def pack_wire(target, frame, chunk, main, rest):
    cols = target.shape[1] * 2 // 3
    target[frame, pl.ds(STEP * chunk, STEP)] = main.astype(target.dtype)
    pair = rest.reshape((STEP // 2, 2) + rest.shape[1:])
    target[frame, pl.ds(cols + STEP // 2 * chunk, STEP // 2)] = (pair[:, 0] + swap_half(pair[:, 1])).astype(target.dtype)


def clear_borders(buf):
    frames, slots, rows, lanes = buf.shape
    for frame in range(frames):
        for slot in (0, slots - 2, slots - 1):
            buf[frame, slot] = jnp.zeros((rows, lanes), buf.dtype)


def store_pieces(buf, frame, chunk, main, rest):
    rows = main.shape[1]
    row = lax.broadcasted_iota(jnp.int32, main.shape, 1)

    def above(value):
        return jnp.where(row == 0, 0.0, pltpu.roll(value, 1, axis=1))

    def below(value):
        return jnp.where(row == rows - 1, 0.0, pltpu.roll(value, rows - 1, axis=1))

    def put(first_slot, lane, value):
        buf[frame, pl.ds(first_slot, STEP), :, lane : lane + value.shape[-1]] = value.astype(buf.dtype)

    slot = STEP * chunk + 1
    put(slot, 0, above(main))
    put(slot, LANES, main)
    put(slot, 2 * LANES, below(main))
    put(slot, 3 * LANES, above(rest) + swap_half(rest))
    lower = below(rest)
    put(slot, 4 * LANES, lower[..., : LANES // 2])
    put(slot - 1, 4 * LANES + LANES // 2, lower[..., : LANES // 2])


def convolve(buf, frame, weight, layer, hidden):
    rows = buf.shape[2]
    cols = buf.shape[1] - 2
    channels = weight.shape[-1]
    span = channels - LANES

    def piece(tap, col, lane):
        return buf[frame + tap, col : col + cols, :, lane : lane + LANES].reshape(cols * rows, LANES)

    def taken(tap, row, col, rest):
        index = (tap * 3 + row) * 3 + col
        return weight[layer, index, LANES:channels, :] if rest else weight[layer, index, 0:LANES, :]

    total = None
    for tap in range(3):
        lhs, rhs = [], []
        for col in range(3):
            for row in range(3):
                lhs.append(piece(tap, col, LANES * row))
                rhs.append(taken(tap, row, col, False))
            lhs.append(piece(tap, col, 3 * LANES))
            rhs += [taken(tap, 0, col, True), taken(tap, 1, col, True)]
        lhs.append(piece(tap, 0, 4 * LANES))
        rhs += [taken(tap, 2, 0, True), taken(tap, 2, 1, True)]
        lhs.append(piece(tap, 2, 4 * LANES))
        rhs += [taken(tap, 2, 2, True), jnp.zeros((span, channels), weight.dtype)]
        part = jnp.dot(
            jnp.concatenate(lhs, axis=1), jnp.concatenate(rhs, axis=0), preferred_element_type=jnp.float32
        )
        total = part if total is None else total + part
    hidden[0] = total[:, :LANES].reshape(cols, rows, LANES)
    hidden[1, :, :, 0:span] = total[:, LANES:].reshape(cols, rows, span)


def each_chunk(cols, body):
    lax.fori_loop(0, cols // STEP, lambda i, carry: (body(i), carry)[1], 0)


def each_frame(count, body):
    lax.fori_loop(0, count, lambda i, carry: (body(i), carry)[1], 0)


def hidden_chunk(hidden, chunk):
    return hidden[0, pl.ds(STEP * chunk, STEP)], hidden[1, pl.ds(STEP * chunk, STEP)]


def own_span(starts, frames):
    span = lax.axis_index("tm")
    own_start, own_frames = starts[0], frames[0]
    for v in range(1, starts.shape[0]):
        here = starts[v] <= span
        own_start = jnp.where(here, starts[v], own_start)
        own_frames = jnp.where(here, frames[v], own_frames)
    return span, own_start, own_frames


def keep_factor(starts, frames):
    span, own_start, _ = own_span(starts, frames)
    return jnp.where(span - 1 >= own_start, 1.0, 0.0).astype(jnp.float32)


def first_kernel(dense, gains, weight_hbm, first, second, wire, weight, hidden, gain_pad, sem):
    copy = pltpu.make_async_copy(weight_hbm.at[pl.ds(0, 1)], weight, sem)
    copy.start()
    cols = first.shape[1] - 2
    channels = gains.shape[1]
    fill_gain(gains, gain_pad)
    clear_borders(first)
    clear_borders(second)
    hidden[1] = jnp.zeros_like(hidden[1])

    def enter(frame):
        def body(chunk):
            main, rest = unpack_dense(dense, frame, chunk)
            main, rest = activate(main, rest, *load_gain(gains, gain_pad, 0), channels)
            store_pieces(first, frame + HALO, chunk, main, rest)

        each_chunk(cols, body)

    each_frame(dense.shape[0], enter)
    copy.wait()
    hidden_out(first, HALO, weight, 0, hidden, gains, gain_pad, 1, second, wire)


def hidden_out(source, base, weight, layer, hidden, gains, gain_pad, gain_index, target, wire):
    cols = source.shape[1] - 2
    channels = gains.shape[1]

    def frame_body(i):
        convolve(source, base + i, weight, layer, hidden)

        def body(chunk):
            main, rest = activate(*hidden_chunk(hidden, chunk), *load_gain(gains, gain_pad, gain_index), channels)
            store_pieces(target, base + HALO + i, chunk, main, rest)
            if wire is not None:
                pack_wire(wire, i, chunk, main, rest)

        each_chunk(cols, body)

    each_frame(HALO, frame_body)


def residual_out(source, base, weight, layer, hidden, finish):
    cols = source.shape[1] - 2

    def frame_body(i):
        convolve(source, base + i, weight, layer, hidden)
        each_chunk(cols, lambda chunk: finish(i, chunk, *hidden_chunk(hidden, chunk)))

    each_frame(HALO, frame_body)


def rounded(value):
    return value.astype(jnp.bfloat16).astype(jnp.float32)


def state_put(state, i, chunk, main, rest):
    state[i, 0, pl.ds(STEP * chunk, STEP)] = main.astype(state.dtype)
    state[i, 1, pl.ds(STEP * chunk, STEP)] = rest.astype(state.dtype)


def state_get(state, i, chunk):
    return (
        state[i, 0, pl.ds(STEP * chunk, STEP)].astype(jnp.float32),
        state[i, 1, pl.ds(STEP * chunk, STEP)].astype(jnp.float32),
    )


def halo_in(wire, target, keep):
    cols = target.shape[1] - 2

    def frame_body(frame):
        each_chunk(cols, lambda chunk: store_pieces(target, frame, chunk, *unpack_wire(wire, frame, chunk, keep)))

    each_frame(HALO, frame_body)


def second_kernel(
    starts, frames, dense_halo, dense, gains, weight, first_in, second_in, first, second, third, state, wire, hidden, gain_pad
):
    cols = first.shape[1] - 2
    channels = gains.shape[1]
    keep = keep_factor(starts, frames)
    fill_gain(gains, gain_pad)
    clear_borders(third)
    hidden[1] = jnp.zeros_like(hidden[1])

    def enter(frame):
        def body(chunk):
            main, rest = unpack_dense(dense_halo, frame, chunk)
            main, rest = activate(main, rest, *load_gain(gains, gain_pad, 0), channels)
            store_pieces(first, frame, chunk, main * keep, rest * keep)

        each_chunk(cols, body)

    each_frame(HALO, enter)
    hidden_out(first, 0, weight, 0, hidden, gains, gain_pad, 1, second, None)

    def finish(i, chunk, main, rest):
        main_in, rest_in = unpack_dense(dense, HALO + i, chunk)
        main, rest = rounded(main + main_in), rounded(rest + rest_in)
        state_put(state, i, chunk, main, rest)
        main, rest = activate(main, rest, *load_gain(gains, gain_pad, 2), channels)
        store_pieces(third, 2 * HALO + i, chunk, main, rest)
        pack_wire(wire, i, chunk, main, rest)

    residual_out(second, HALO, weight, 1, hidden, finish)


def third_kernel(
    starts, frames, halo, dense, gains, weight, second_in, third_in, second, third, fourth, state, wire, hidden, gain_pad
):
    channels = gains.shape[1]
    keep = keep_factor(starts, frames)
    fill_gain(gains, gain_pad)
    clear_borders(fourth)
    hidden[1] = jnp.zeros_like(hidden[1])
    halo_in(halo, second, keep)

    def finish(i, chunk, main, rest):
        main_in, rest_in = unpack_dense(dense, i, chunk)
        main, rest = rounded(main + main_in), rounded(rest + rest_in)
        state_put(state, i, chunk, main, rest)
        main, rest = activate(main, rest, *load_gain(gains, gain_pad, 2), channels)
        store_pieces(third, HALO + i, chunk, main, rest)

    residual_out(second, 0, weight, 1, hidden, finish)
    hidden_out(third, HALO, weight, 2, hidden, gains, gain_pad, 3, fourth, wire)


def live_factor(starts, frames, frame, span_frames):
    span, own_start, own_frames = own_span(starts, frames)
    return jnp.where((span - own_start) * span_frames + frame < own_frames, 1.0, 0.0).astype(jnp.float32)


def fourth_kernel(
    starts, frames, halo, gains, weight, third_in, fourth_in, state, third, fourth, out, hidden, gain_pad
):
    keep = keep_factor(starts, frames)
    fill_gain(gains, gain_pad)
    hidden[1] = jnp.zeros_like(hidden[1])
    halo_in(halo, third, keep)
    hidden_out(third, 0, weight, 2, hidden, gains, gain_pad, 3, fourth, None)

    def finish(i, chunk, main, rest):
        main_in, rest_in = state_get(state, i, chunk)
        live = live_factor(starts, frames, HALO + i, 2 * HALO)
        pack_dense(out, i, chunk, (main + main_in) * live, (rest + rest_in) * live)

    residual_out(fourth, HALO, weight, 3, hidden, finish)


def fifth_kernel(starts, frames, halo, weight, fourth_in, state, later, fourth, out, hidden):
    keep = keep_factor(starts, frames)
    hidden[1] = jnp.zeros_like(hidden[1])
    halo_in(halo, fourth, keep)
    out[HALO:] = later[...]

    def finish(i, chunk, main, rest):
        main_in, rest_in = state_get(state, i, chunk)
        live = live_factor(starts, frames, i, 2 * HALO)
        pack_dense(out, i, chunk, (main + main_in) * live, (rest + rest_in) * live)

    residual_out(fourth, 0, weight, 3, hidden, finish)


def local(features, gains, conv_weights, video_frames, video_start):
    frames, rows, merged = features.shape
    channels = gains.shape[1]
    cols = merged // channels
    layers = conv_weights.shape[0]
    weight = conv_weights.reshape(layers, 27, channels, channels)
    bf16, f32 = jnp.bfloat16, jnp.float32
    pieces = jax.ShapeDtypeStruct((frames + HALO, cols + 2, rows, 5 * LANES), bf16)
    wire = jax.ShapeDtypeStruct((HALO, cols * 3 // 2, rows, LANES), bf16)
    state = jax.ShapeDtypeStruct((HALO, 2, cols, rows, LANES), bf16)
    hidden = VMEM((2, cols, rows, LANES), f32)
    gain_pad = VMEM((layers, 2, LANES), f32)
    smem = pl.BlockSpec(memory_space=pltpu.SMEM)
    vmem = pl.BlockSpec(memory_space=VMEM)
    hbm = pl.BlockSpec(memory_space=pltpu.HBM)

    def call(body, ins, outs, scratch, convs, aliases=None, name=None):
        return pl.pallas_call(
            body,
            out_shape=outs,
            in_specs=ins,
            out_specs=tuple(vmem for _ in outs),
            scratch_shapes=scratch,
            input_output_aliases=aliases or {},
            name=name,
            compiler_params=pltpu.CompilerParams(vmem_limit_bytes=12 << 20),
            cost_estimate=pl.CostEstimate(
                flops=convs * 2 * 27 * channels * channels * rows * cols * 2,
                bytes_accessed=4 << 20,
                transcendentals=0,
            ),
        )

    halo0 = passed_along(features[frames - HALO :], "tm")
    first, second, wire1 = call(
        first_kernel,
        [vmem, vmem, hbm],
        (pieces, pieces, wire),
        [VMEM((1, 27, channels, channels), bf16), hidden, gain_pad, pltpu.SemaphoreType.DMA],
        1,
        name="k1",
    )(features, gains, weight)
    halo1 = passed_along(wire1, "tm")
    _, second, third, state_late, wire2 = call(
        second_kernel,
        [smem, smem] + [vmem] * 6,
        (pieces, pieces, pieces, state, wire),
        [hidden, gain_pad],
        2,
        {6: 0, 7: 1},
        name="k2",
    )(video_start, video_frames, halo0, features, gains, weight, first, second)
    halo2 = passed_along(wire2, "tm")
    _, third, fourth, state_early, wire3 = call(
        third_kernel,
        [smem, smem] + [vmem] * 6,
        (pieces, pieces, pieces, state, wire),
        [hidden, gain_pad],
        2,
        {6: 0, 7: 1},
        name="k3",
    )(video_start, video_frames, halo1, features, gains, weight, second, third)
    halo3 = passed_along(wire3, "tm")
    dense_half = jax.ShapeDtypeStruct((HALO, rows, merged), bf16)
    _, fourth, later = call(
        fourth_kernel,
        [smem, smem] + [vmem] * 6,
        (pieces, pieces, dense_half),
        [hidden, gain_pad],
        2,
        {5: 0, 6: 1},
        name="k4",
    )(video_start, video_frames, halo2, gains, weight, third, fourth, state_late)
    _, out = call(
        fifth_kernel,
        [smem, smem] + [vmem] * 5,
        (pieces, jax.ShapeDtypeStruct(features.shape, bf16)),
        [hidden],
        1,
        {4: 0},
        name="k5",
    )(video_start, video_frames, halo3, weight, fourth, state_early, later)
    return out


def solution(mesh):
    in_specs = (P(("grp", "tm"), None, None), P(), P(), P("grp"), P("grp"))
    out_specs = P(("grp", "tm"), None, None)
    return jax.shard_map(local, mesh=mesh, in_specs=in_specs, out_specs=out_specs, check_vma=False)
```

profile of v0, /device:TPU:0, one launch (start us, length us, event | category | flops | bytes accessed | tf_op | source)
XLA Modules:
  0.0 74.3 jit_solution(13306773460901556351)
XLA Ops:
  0.0 1.0 %slice.3 = bf16[2,16,4608]{2,1,0:T(8,128)(2,1)S(1)} slice(bf16[4,16,4608]{2,1,0:T(8,128)(2,1)} %dense.5), slice={[2:4], [0:16], [0:4608]} | slice | bytes 589824 | tf_op jit(solution)/shard_map/slice | solution.py:384
  1.0 2.4 %collective-permute-start.1 = (bf16[2,16,4608]{2,1,0:T(8,128)(2,1)S(1)}, bf16[2,16,4608]{2,1,0:T(8,128)(2,1)S(1)}, u32[]{:S(2)}, u32[]{:S(2)}) collective-permute-start(bf16[2,16,4608]{2,1,0:T(8,128)(2,1)S(1)} %slice.3), channel_id=1, source_target_pairs={{0,1},{1,2},{2,3},{3,4},{4,5},{5,6},{6,7},{7,8},{8,9},{9,10},{10,1... | collective-permute-start | bytes 884744 | tf_op jit(solution)/shard_map/ppermute | solution.py:18
  3.4 0.0 copy-start
  3.4 4.0 %copy-done = bf16[4,3,3,3,192,192]{5,4,3,2,1,0:T(8,128)(2,1)S(1)} copy-done((bf16[4,3,3,3,192,192]{5,4,3,2,1,0:T(8,128)(2,1)S(1)}, bf16[4,3,3,3,192,192]{5,4,3,2,1,0:T(8,128)(2,1)}, u32[]{:S(2)}) %copy-start) | copy-done | bytes 7962648
  7.4 0.0 copy-start.1
  7.4 1.1 %copy-done.1 = bf16[4,16,4608]{2,1,0:T(8,128)(2,1)S(1)} copy-done((bf16[4,16,4608]{2,1,0:T(8,128)(2,1)S(1)}, bf16[4,16,4608]{2,1,0:T(8,128)(2,1)}, u32[]{:S(2)}) %copy-start.1) | copy-done | bytes 589848
  8.5 0.0 copy-start.2
  8.5 0.7 copy-done.2
  9.2 0.0 copy-start.3
  9.2 0.0 copy-start.4
  9.2 11.1 %k1.1 = (bf16[6,26,16,640]{3,2,1,0:T(8,128)(2,1)S(1)}, bf16[6,26,16,640]{3,2,1,0:T(8,128)(2,1)S(1)}, bf16[2,36,16,128]{3,2,1,0:T(8,128)(2,1)S(1)}) custom-call(bf16[4,16,4608]{2,1,0:T(8,128)(2,1)S(1)} %copy-done.1, f32[4,192]{1,0:T(4,128)S(1)} %copy-done.2, bf16[4,27,192,192]{3,2,1,0:T(8,128)(2,1)S(1)} %bitcast.1), custom_call_target="tpu_custom_call" | custom-call | flops 1528823808 | bytes 4194304 | tf_op jit(solution)/shard_map/k1/pallas_call | solution.py:385
  20.3 4.5 %collective-permute-start = (bf16[2,36,16,128]{3,2,1,0:T(8,128)(2,1)S(1)}, bf16[2,36,16,128]{3,2,1,0:T(8,128)(2,1)S(1)}, u32[]{:S(2)}, u32[]{:S(2)}) collective-permute-start(bf16[2,36,16,128]{3,2,1,0:T(8,128)(2,1)S(1)} %get-tuple-element.19), channel_id=1, source_target_pairs={{0,1},{1,2},{2,3},{3,4},{4,5},{5,6},{6,7},{7,8},{8,9},{9,10},{10,1... | collective-permute-start | bytes 884744 | tf_op jit(solution)/shard_map/ppermute | solution.py:18
  24.8 0.0 collective-permute-done.1.dense_halo
  24.8 0.0 copy-done.3
  24.8 0.0 copy-done.4
  24.8 0.0 slice-start
  24.8 0.0 slice-start.1
  24.9 13.9 %k2.1 = (bf16[6,26,16,640]{3,2,1,0:T(8,128)(2,1)S(1)}, bf16[6,26,16,640]{3,2,1,0:T(8,128)(2,1)S(1)}, bf16[6,26,16,640]{3,2,1,0:T(8,128)(2,1)S(1)}, bf16[2,2,24,1...) custom-call(s32[4]{0:T(128)S(1)} %copy-done.3, ...), custom_call_target="tpu_custom_call", output_to_operand_aliasing={{0}: (6, {}), {1}: (7, {})} | custom-call | flops 3057647616 | bytes 4194304 | tf_op jit(solution)/shard_map/k2/pallas_call | solution.py:394
  38.8 1.9 %collective-permute-start.3 = (bf16[2,36,16,128]{3,2,1,0:T(8,128)(2,1)S(1)}, bf16[2,36,16,128]{3,2,1,0:T(8,128)(2,1)S(1)}, u32[]{:S(2)}, u32[]{:S(2)}) collective-permute-start(bf16[2,36,16,128]{3,2,1,0:T(8,128)(2,1)S(1)} %get-tuple-element.25), channel_id=1, source_target_pairs={{0,1},{1,2},{2,3},{3,4},{4,5},{5,6},{6,7},{7,8},{8,9},{9,10},{10,1... | collective-permute-start | bytes 884744 | tf_op jit(solution)/shard_map/ppermute | solution.py:18
  40.7 0.0 collective-permute-done.halo
  40.7 0.0 slice-start.2
  40.7 12.7 %k3.1 = (bf16[6,26,16,640]{3,2,1,0:T(8,128)(2,1)S(1)}, bf16[6,26,16,640]{3,2,1,0:T(8,128)(2,1)S(1)}, bf16[6,26,16,640]{3,2,1,0:T(8,128)(2,1)S(1)}, bf16[2,2,24,1...) custom-call(s32[4]{0:T(128)S(1)} %copy-done.3, ...), custom_call_target="tpu_custom_call", output_to_operand_aliasing={{0}: (6, {}), {1}: (7, {})} | custom-call | flops 3057647616 | bytes 4194304 | tf_op jit(solution)/shard_map/k3/pallas_call | solution.py:404
  53.5 3.5 %collective-permute-start.2 = (bf16[2,36,16,128]{3,2,1,0:T(8,128)(2,1)S(1)}, bf16[2,36,16,128]{3,2,1,0:T(8,128)(2,1)S(1)}, u32[]{:S(2)}, u32[]{:S(2)}) collective-permute-start(bf16[2,36,16,128]{3,2,1,0:T(8,128)(2,1)S(1)} %get-tuple-element.24), channel_id=1, source_target_pairs={{0,1},{1,2},{2,3},{3,4},{4,5},{5,6},{6,7},{7,8},{8,9},{9,10},{10,1... | collective-permute-start | bytes 884744 | tf_op jit(solution)/shard_map/ppermute | solution.py:18
  57.0 0.0 collective-permute-done.3.halo
  57.0 0.0 slice-done
  57.0 0.0 slice-done.1
  57.0 0.0 slice-done.2
  57.0 10.6 %k4.1 = (bf16[6,26,16,640]{3,2,1,0:T(8,128)(2,1)S(1)}, bf16[6,26,16,640]{3,2,1,0:T(8,128)(2,1)S(1)}, bf16[2,16,4608]{2,1,0:T(8,128)(2,1)S(1)}) custom-call(s32[4]{0:T(128)S(1)} %copy-done.3, s32[4]{0:T(128)S(1)} %copy-done.4, bf16[2,36,16,128]{3,2,1,0:T(8,128)(2,1)S(1)} %collective-permute-done.3.halo, ...), custom_call_target="tpu_custom_call", output_to_operand_aliasing={{0}: (5, {}), {1}: (6, {})} | custom-call | flops 3057647616 | bytes 4194304 | tf_op jit(solution)/shard_map/k4/pallas_call | solution.py:415
  67.7 0.0 collective-permute-done.2.halo
  67.7 6.7 %k5.1 = (bf16[6,26,16,640]{3,2,1,0:T(8,128)(2,1)S(1)}, bf16[4,16,4608]{2,1,0:T(8,128)(2,1)}) custom-call(s32[4]{0:T(128)S(1)} %copy-done.3, s32[4]{0:T(128)S(1)} %copy-done.4, bf16[2,36,16,128]{3,2,1,0:T(8,128)(2,1)S(1)} %collective-permute-done.2.halo, bf16[4,27,192,192]{3,2,1,0:T(8,128)(2,1)S(1)} %bitcast.7, ...), custom_call_target="tpu_custom_call", output_to_operand_aliasing={{0}: (4, {})} | custom-call | flops 1528823808 | bytes 4194304 | tf_op jit(solution)/shard_map/k5/pallas_call | solution.py:424
  (1 shorter events, 0.0 us)
Async XLA Ops:
  1.0 23.8 %collective-permute-start.1 = (bf16[2,16,4608]{2,1,0:T(8,128)(2,1)S(1)}, bf16[2,16,4608]{2,1,0:T(8,128)(2,1)S(1)}, u32[]{:S(2)}, u32[]{:S(2)}) collective-permute-start(bf16[2,16,4608]{2,1,0:T(8,128)(2,1)S(1)} %slice.3), channel_id=1, source_target_pairs={{0,1},{1,2},{2,3},{3,4},{4,5},{5,6},{6,7},{7,8},{8,9},{9,10},{10,1... | collective-permute-start | bytes 884744 | tf_op jit(solution)/shard_map/ppermute | solution.py:18
  3.4 4.0 %copy-start = (bf16[4,3,3,3,192,192]{5,4,3,2,1,0:T(8,128)(2,1)S(1)}, bf16[4,3,3,3,192,192]{5,4,3,2,1,0:T(8,128)(2,1)}, u32[]{:S(2)}) copy-start(bf16[4,3,3,3,192,192]{5,4,3,2,1,0:T(8,128)(2,1)} %param.7) | copy-start | bytes 23887876
  7.4 1.1 %copy-start.1 = (bf16[4,16,4608]{2,1,0:T(8,128)(2,1)S(1)}, bf16[4,16,4608]{2,1,0:T(8,128)(2,1)}, u32[]{:S(2)}) copy-start(bf16[4,16,4608]{2,1,0:T(8,128)(2,1)} %dense.5) | copy-start | bytes 1769476
  8.5 0.7 copy-start.2
  9.2 15.6 %copy-start.3 = (s32[4]{0:T(128)S(1)}, s32[4]{0:T(128)}, u32[]{:S(2)}) copy-start(s32[4]{0:T(128)} %starts.7) | copy-start | bytes 52
  9.2 15.6 %copy-start.4 = (s32[4]{0:T(128)S(1)}, s32[4]{0:T(128)}, u32[]{:S(2)}) copy-start(s32[4]{0:T(128)} %frames.7) | copy-start | bytes 52
  20.3 20.4 %collective-permute-start = (bf16[2,36,16,128]{3,2,1,0:T(8,128)(2,1)S(1)}, bf16[2,36,16,128]{3,2,1,0:T(8,128)(2,1)S(1)}, u32[]{:S(2)}, u32[]{:S(2)}) collective-permute-start(bf16[2,36,16,128]{3,2,1,0:T(8,128)(2,1)S(1)} %get-tuple-element.19), channel_id=1, source_target_pairs={{0,1},{1,2},{2,3},{3,4},{4,5},{5,6},{6,7},{7,8},{8,9},{9,10},{10,1... | collective-permute-start | bytes 884744 | tf_op jit(solution)/shard_map/ppermute | solution.py:18
  24.8 32.2 %slice-start = ((s8[10616832]{0:T(1024)(128)(4,1)}), s8[4194304]{0:T(1024)(128)(4,1)S(1)}, s32[]{:S(2)}) async-start(s8[10616832]{0:T(1024)(128)(4,1)} %bitcast.4), calls=%async_computation | async-start | bytes 8388608
  24.8 32.2 %slice-start.1 = ((s8[10616832]{0:T(1024)(128)(4,1)}), s8[4194304]{0:T(1024)(128)(4,1)S(1)}, s32[]{:S(2)}) async-start(s8[10616832]{0:T(1024)(128)(4,1)} %bitcast.4), calls=%async_computation.1 | async-start | bytes 8388608
  38.8 18.2 %collective-permute-start.3 = (bf16[2,36,16,128]{3,2,1,0:T(8,128)(2,1)S(1)}, bf16[2,36,16,128]{3,2,1,0:T(8,128)(2,1)S(1)}, u32[]{:S(2)}, u32[]{:S(2)}) collective-permute-start(bf16[2,36,16,128]{3,2,1,0:T(8,128)(2,1)S(1)} %get-tuple-element.25), channel_id=1, source_target_pairs={{0,1},{1,2},{2,3},{3,4},{4,5},{5,6},{6,7},{7,8},{8,9},{9,10},{10,1... | collective-permute-start | bytes 884744 | tf_op jit(solution)/shard_map/ppermute | solution.py:18
  40.7 16.3 %slice-start.2 = ((s8[10616832]{0:T(1024)(128)(4,1)}), s8[2228224]{0:T(1024)(128)(4,1)S(1)}, s32[]{:S(2)}) async-start(s8[10616832]{0:T(1024)(128)(4,1)} %bitcast.4), calls=%async_computation.2 | async-start | bytes 4456448
  53.5 14.2 %collective-permute-start.2 = (bf16[2,36,16,128]{3,2,1,0:T(8,128)(2,1)S(1)}, bf16[2,36,16,128]{3,2,1,0:T(8,128)(2,1)S(1)}, u32[]{:S(2)}, u32[]{:S(2)}) collective-permute-start(bf16[2,36,16,128]{3,2,1,0:T(8,128)(2,1)S(1)} %get-tuple-element.24), channel_id=1, source_target_pairs={{0,1},{1,2},{2,3},{3,4},{4,5},{5,6},{6,7},{7,8},{8,9},{9,10},{10,1... | collective-permute-start | bytes 884744 | tf_op jit(solution)/shard_map/ppermute | solution.py:18
where the time goes:
time: 74.7 us; the launch traced here: 74.3 us
  Pallas kernels  55 us (74%)
  starting transfers between devices  12.4 us (17%)
  local copies, waits for them, and re-layouts  6.77 us (9%)
    pallas_call x1, Pallas kernels, local(): call(second_kernel, [smem, smem] + [vmem] * 6, (pieces, pieces, pieces, s...  13.9 us
    pallas_call x1, Pallas kernels, local(): call(third_kernel, [smem, smem] + [vmem] * 6, (pieces, pieces, pieces, st...  12.7 us
    ppermute x4, starting transfers between devices, passed_along(): return lax.ppermute(value, axis, [(i, i + 1) for i in range(count - 1)])  12.4 us
    pallas_call x1, Pallas kernels, local(): call(first_kernel, [vmem, vmem, hbm], (pieces, pieces, wire), [VMEM((1, 2...  11.1 us
    pallas_call x1, Pallas kernels, local(): call(fourth_kernel, [smem, smem] + [vmem] * 6, (pieces, pieces, dense_hal...  10.6 us
    pallas_call x1, Pallas kernels, local(): call(fifth_kernel, [smem, smem] + [vmem] * 5, (pieces, jax.ShapeDtypeStru...  6.67 us
    unnamed x16, local copies, waits for them, and re-layouts  5.79 us
  transfers between devices with their start and end apart: 4, of which 0 were waited for; matrix products, arithmetic and copies ran while one was open for 0% of the time, Pallas kernels for 65%

commit v1 on v0

--- a/solution.py
+++ b/solution.py
@@ -53,7 +53,7 @@
 def unpack_dense(source, frame, chunk):
     rows = source.shape[1]
     width = STEP * 192
-    block = source[frame, :, pl.ds(pl.multiple_of(chunk * width, LANES), width)].astype(jnp.float32)
+    block = source[frame, :, chunk * width : (chunk + 1) * width].astype(jnp.float32)
     tile = [block[:, LANES * i : LANES * (i + 1)] for i in range(width // LANES)]
     low = low_half((rows, LANES))
     main, rest = [], []
@@ -73,7 +73,7 @@
         rolled = swap_half(main[i + 1])
         tile += [main[i], jnp.where(low, rest[i], rolled), jnp.where(low, rolled, swap_half(rest[i + 1]))]
     block = jnp.concatenate(tile, axis=-1).astype(target.dtype)
-    target[frame, :, pl.ds(pl.multiple_of(chunk * width, LANES), width)] = block
+    target[frame, :, chunk * width : (chunk + 1) * width] = block
 
 
 def unpack_wire(source, frame, chunk, keep):
@@ -122,7 +122,7 @@
     put(slot - 1, 4 * LANES + LANES // 2, lower[..., : LANES // 2])
 
 
-def convolve(buf, frame, weight, layer, hidden):
+def convolve(buf, frame, weight, layer, hidden, slot):
     rows = buf.shape[2]
     cols = buf.shape[1] - 2
     channels = weight.shape[-1]
@@ -135,9 +135,8 @@
         index = (tap * 3 + row) * 3 + col
         return weight[layer, index, LANES:channels, :] if rest else weight[layer, index, 0:LANES, :]
 
-    total = None
-    for tap in range(3):
-        lhs, rhs = [], []
+    lhs, rhs = [], []
+    for tap in (2, 1, 0):
         for col in range(3):
             for row in range(3):
                 lhs.append(piece(tap, col, LANES * row))
@@ -148,24 +147,23 @@
         rhs += [taken(tap, 2, 0, True), taken(tap, 2, 1, True)]
         lhs.append(piece(tap, 2, 4 * LANES))
         rhs += [taken(tap, 2, 2, True), jnp.zeros((span, channels), weight.dtype)]
-        part = jnp.dot(
-            jnp.concatenate(lhs, axis=1), jnp.concatenate(rhs, axis=0), preferred_element_type=jnp.float32
-        )
-        total = part if total is None else total + part
-    hidden[0] = total[:, :LANES].reshape(cols, rows, LANES)
-    hidden[1, :, :, 0:span] = total[:, LANES:].reshape(cols, rows, span)
+    total = jnp.dot(jnp.concatenate(lhs, axis=1), jnp.concatenate(rhs, axis=0), preferred_element_type=jnp.float32)
+    hidden[slot, 0] = total[:, :LANES].reshape(cols, rows, LANES)
+    hidden[slot, 1, :, :, 0:span] = total[:, LANES:].reshape(cols, rows, span)
 
 
 def each_chunk(cols, body):
-    lax.fori_loop(0, cols // STEP, lambda i, carry: (body(i), carry)[1], 0)
+    for chunk in range(cols // STEP):
+        body(chunk)
 
 
 def each_frame(count, body):
-    lax.fori_loop(0, count, lambda i, carry: (body(i), carry)[1], 0)
-
-
-def hidden_chunk(hidden, chunk):
-    return hidden[0, pl.ds(STEP * chunk, STEP)], hidden[1, pl.ds(STEP * chunk, STEP)]
+    for index in range(count):
+        body(index)
+
+
+def hidden_chunk(hidden, slot, chunk):
+    return hidden[slot, 0, pl.ds(STEP * chunk, STEP)], hidden[slot, 1, pl.ds(STEP * chunk, STEP)]
 
 
 def own_span(starts, frames):
@@ -183,15 +181,22 @@
     return jnp.where(span - 1 >= own_start, 1.0, 0.0).astype(jnp.float32)
 
 
-def first_kernel(dense, gains, weight_hbm, first, second, wire, weight, hidden, gain_pad, sem):
-    copy = pltpu.make_async_copy(weight_hbm.at[pl.ds(0, 1)], weight, sem)
-    copy.start()
+def first_kernel(dense_hbm, gains_hbm, weight_hbm, first, second, wire, dense, gains, weight, hidden, gain_pad, sems):
+    copies = [
+        pltpu.make_async_copy(gains_hbm, gains, sems.at[0]),
+        pltpu.make_async_copy(dense_hbm, dense, sems.at[1]),
+        pltpu.make_async_copy(weight_hbm.at[pl.ds(0, 1)], weight, sems.at[2]),
+    ]
+    for copy in copies:
+        copy.start()
     cols = first.shape[1] - 2
     channels = gains.shape[1]
-    fill_gain(gains, gain_pad)
     clear_borders(first)
     clear_borders(second)
-    hidden[1] = jnp.zeros_like(hidden[1])
+    hidden[:, 1] = jnp.zeros_like(hidden[:, 1])
+    copies[0].wait()
+    fill_gain(gains, gain_pad)
+    copies[1].wait()
 
     def enter(frame):
         def body(chunk):
@@ -202,7 +207,7 @@
         each_chunk(cols, body)
 
     each_frame(dense.shape[0], enter)
-    copy.wait()
+    copies[2].wait()
     hidden_out(first, HALO, weight, 0, hidden, gains, gain_pad, 1, second, wire)
 
 
@@ -211,10 +216,10 @@
     channels = gains.shape[1]
 
     def frame_body(i):
-        convolve(source, base + i, weight, layer, hidden)
+        convolve(source, base + i, weight, layer, hidden, 2 * (layer % 2) + i)
 
         def body(chunk):
-            main, rest = activate(*hidden_chunk(hidden, chunk), *load_gain(gains, gain_pad, gain_index), channels)
+            main, rest = activate(*hidden_chunk(hidden, 2 * (layer % 2) + i, chunk), *load_gain(gains, gain_pad, gain_index), channels)
             store_pieces(target, base + HALO + i, chunk, main, rest)
             if wire is not None:
                 pack_wire(wire, i, chunk, main, rest)
@@ -228,8 +233,8 @@
     cols = source.shape[1] - 2
 
     def frame_body(i):
-        convolve(source, base + i, weight, layer, hidden)
-        each_chunk(cols, lambda chunk: finish(i, chunk, *hidden_chunk(hidden, chunk)))
+        convolve(source, base + i, weight, layer, hidden, 2 * (layer % 2) + i)
+        each_chunk(cols, lambda chunk: finish(i, chunk, *hidden_chunk(hidden, 2 * (layer % 2) + i, chunk)))
 
     each_frame(HALO, frame_body)
 
@@ -267,7 +272,7 @@
     keep = keep_factor(starts, frames)
     fill_gain(gains, gain_pad)
     clear_borders(third)
-    hidden[1] = jnp.zeros_like(hidden[1])
+    hidden[:, 1] = jnp.zeros_like(hidden[:, 1])
 
     def enter(frame):
         def body(chunk):
@@ -298,7 +303,7 @@
     keep = keep_factor(starts, frames)
     fill_gain(gains, gain_pad)
     clear_borders(fourth)
-    hidden[1] = jnp.zeros_like(hidden[1])
+    hidden[:, 1] = jnp.zeros_like(hidden[:, 1])
     halo_in(halo, second, keep)
 
     def finish(i, chunk, main, rest):
@@ -322,7 +327,7 @@
 ):
     keep = keep_factor(starts, frames)
     fill_gain(gains, gain_pad)
-    hidden[1] = jnp.zeros_like(hidden[1])
+    hidden[:, 1] = jnp.zeros_like(hidden[:, 1])
     halo_in(halo, third, keep)
     hidden_out(third, 0, weight, 2, hidden, gains, gain_pad, 3, fourth, None)
 
@@ -336,7 +341,7 @@
 
 def fifth_kernel(starts, frames, halo, weight, fourth_in, state, later, fourth, out, hidden):
     keep = keep_factor(starts, frames)
-    hidden[1] = jnp.zeros_like(hidden[1])
+    hidden[:, 1] = jnp.zeros_like(hidden[:, 1])
     halo_in(halo, fourth, keep)
     out[HALO:] = later[...]
 
@@ -358,7 +363,7 @@
     pieces = jax.ShapeDtypeStruct((frames + HALO, cols + 2, rows, 5 * LANES), bf16)
     wire = jax.ShapeDtypeStruct((HALO, cols * 3 // 2, rows, LANES), bf16)
     state = jax.ShapeDtypeStruct((HALO, 2, cols, rows, LANES), bf16)
-    hidden = VMEM((2, cols, rows, LANES), f32)
+    hidden = VMEM((2 * HALO, 2, cols, rows, LANES), f32)
     gain_pad = VMEM((layers, 2, LANES), f32)
     smem = pl.BlockSpec(memory_space=pltpu.SMEM)
     vmem = pl.BlockSpec(memory_space=VMEM)
@@ -384,12 +389,19 @@
     halo0 = passed_along(features[frames - HALO :], "tm")
     first, second, wire1 = call(
         first_kernel,
-        [vmem, vmem, hbm],
+        [hbm, hbm, hbm],
         (pieces, pieces, wire),
-        [VMEM((1, 27, channels, channels), bf16), hidden, gain_pad, pltpu.SemaphoreType.DMA],
+        [
+            VMEM(features.shape, bf16),
+            VMEM(gains.shape, f32),
+            VMEM((1, 27, channels, channels), bf16),
+            hidden,
+            gain_pad,
+            pltpu.SemaphoreType.DMA((3,)),
+        ],
         1,
         name="k1",
-    )(features, gains, weight)
+    )(*(pltpu.with_memory_space_constraint(a, pltpu.HBM) for a in (features, gains, weight)))
     halo1 = passed_along(wire1, "tm")
     _, second, third, state_late, wire2 = call(
         second_kernel,

time: 74.7 us -> 43 us (0.58)
  Pallas kernels: 55 us -> 29 us
  local copies, waits for them, and re-layouts: 6.77 us -> 1.01 us
    pallas_call x1, Pallas kernels: 13.9 us -> 5.99 us  [local(): call(second_kernel, [smem, smem] + [vmem] * 6, (pieces, pieces, pieces, s...]
    pallas_call x1, Pallas kernels: 12.7 us -> 5.79 us  [local(): call(third_kernel, [smem, smem] + [vmem] * 6, (pieces, pieces, pieces, st...]
    unnamed x16 -> x10, local copies, waits for them, and re-layouts: 5.79 us -> 0.03 us
    pallas_call x1, Pallas kernels: 10.6 us -> 5.34 us  [local(): call(fourth_kernel, [smem, smem] + [vmem] * 6, (pieces, pieces, dense_hal...]
    pallas_call x1, Pallas kernels: 11.1 us -> 8.1 us  [local(): call(first_kernel, [hbm, hbm, hbm], (pieces, pieces, wire), [VMEM(feature...]
    pallas_call x1, Pallas kernels: 6.67 us -> 3.77 us  [local(): call(fifth_kernel, [smem, smem] + [vmem] * 5, (pieces, jax.ShapeDtypeStru...]
  transfers between devices with their start and end apart: 4 -> 4, of which waited for: 0 -> 0; matrix products, arithmetic and copies ran while one was open for 0% -> 0% of each run, Pallas kernels for 65% -> 59%
where the time goes in v1:
time: 43 us; the launch traced here: 42.8 us
  Pallas kernels  29 us (67%)
  starting transfers between devices  12.6 us (29%)
  local copies, waits for them, and re-layouts  1.01 us (2%)
    ppermute x4, starting transfers between devices, passed_along(): return lax.ppermute(value, axis, [(i, i + 1) for i in range(count - 1)])  12.6 us
    pallas_call x1, Pallas kernels, local(): call(first_kernel, [hbm, hbm, hbm], (pieces, pieces, wire), [VMEM(feature...  8.1 us
    pallas_call x1, Pallas kernels, local(): call(second_kernel, [smem, smem] + [vmem] * 6, (pieces, pieces, pieces, s...  5.99 us
    pallas_call x1, Pallas kernels, local(): call(third_kernel, [smem, smem] + [vmem] * 6, (pieces, pieces, pieces, st...  5.79 us
    pallas_call x1, Pallas kernels, local(): call(fourth_kernel, [smem, smem] + [vmem] * 6, (pieces, pieces, dense_hal...  5.34 us
    pallas_call x1, Pallas kernels, local(): call(fifth_kernel, [smem, smem] + [vmem] * 5, (pieces, jax.ShapeDtypeStru...  3.77 us
    slice x1, local copies, waits for them, and re-layouts, local(): halo0 = passed_along(features[frames - HALO:], 'tm')  0.98 us
  transfers between devices with their start and end apart: 4, of which 0 were waited for; matrix products, arithmetic and copies ran while one was open for 0% of the time, Pallas kernels for 59%

profile of v1, /device:TPU:0, one launch (start us, length us, event | category | flops | bytes accessed | tf_op | source)
XLA Modules:
  0.0 42.8 jit_solution(4920659709727463573)
XLA Ops:
  0.0 1.0 %slice.3 = bf16[2,16,4608]{2,1,0:T(8,128)(2,1)S(1)} slice(bf16[4,16,4608]{2,1,0:T(8,128)(2,1)} %dense.3), slice={[2:4], [0:16], [0:4608]} | slice | bytes 589824 | tf_op jit(solution)/shard_map/slice | solution.py:389
  1.0 2.4 %collective-permute-start.1 = (bf16[2,16,4608]{2,1,0:T(8,128)(2,1)S(1)}, bf16[2,16,4608]{2,1,0:T(8,128)(2,1)S(1)}, u32[]{:S(2)}, u32[]{:S(2)}) collective-permute-start(bf16[2,16,4608]{2,1,0:T(8,128)(2,1)S(1)} %slice.3), channel_id=1, source_target_pairs={{0,1},{1,2},{2,3},{3,4},{4,5},{5,6},{6,7},{7,8},{8,9},{9,10},{10,1... | collective-permute-start | bytes 884744 | tf_op jit(solution)/shard_map/ppermute | solution.py:18
  3.4 0.0 copy-start
  3.4 0.0 copy-start.1
  3.4 0.0 copy-start.2
  3.4 0.0 copy-start.3
  3.5 0.0 copy-start.4
  3.5 8.1 %k1.1 = (bf16[6,26,16,640]{3,2,1,0:T(8,128)(2,1)S(1)}, bf16[6,26,16,640]{3,2,1,0:T(8,128)(2,1)S(1)}, bf16[2,36,16,128]{3,2,1,0:T(8,128)(2,1)S(1)}) custom-call(bf16[4,16,4608]{2,1,0:T(8,128)(2,1)} %dense.3, f32[4,192]{1,0:T(4,128)} %gains.5, bf16[4,27,192,192]{3,2,1,0:T(8,128)(2,1)} %bitcast.1), custom_call_target="tpu_custom_call" | custom-call | flops 1528823808 | bytes 4194304 | tf_op jit(solution)/shard_map/k1/pallas_call | solution.py:390
  11.6 4.5 %collective-permute-start = (bf16[2,36,16,128]{3,2,1,0:T(8,128)(2,1)S(1)}, bf16[2,36,16,128]{3,2,1,0:T(8,128)(2,1)S(1)}, u32[]{:S(2)}, u32[]{:S(2)}) collective-permute-start(bf16[2,36,16,128]{3,2,1,0:T(8,128)(2,1)S(1)} %get-tuple-element.19), channel_id=1, source_target_pairs={{0,1},{1,2},{2,3},{3,4},{4,5},{5,6},{6,7},{7,8},{8,9},{9,10},{10,1... | collective-permute-start | bytes 884744 | tf_op jit(solution)/shard_map/ppermute | solution.py:18
  16.1 0.0 collective-permute-done.1.dense_halo
  16.1 0.0 copy-done
  16.1 0.0 copy-done.1
  16.1 0.0 copy-done.2
  16.1 0.0 copy-done.3
  16.2 0.0 copy-done.4
  16.2 6.0 %k2.1 = (bf16[6,26,16,640]{3,2,1,0:T(8,128)(2,1)S(1)}, bf16[6,26,16,640]{3,2,1,0:T(8,128)(2,1)S(1)}, bf16[6,26,16,640]{3,2,1,0:T(8,128)(2,1)S(1)}, bf16[2,2,24,1...) custom-call(s32[4]{0:T(128)S(1)} %copy-done.3, ...), custom_call_target="tpu_custom_call", output_to_operand_aliasing={{0}: (6, {}), {1}: (7, {})} | custom-call | flops 3057647616 | bytes 4194304 | tf_op jit(solution)/shard_map/k2/pallas_call | solution.py:406
  22.2 2.1 %collective-permute-start.3 = (bf16[2,36,16,128]{3,2,1,0:T(8,128)(2,1)S(1)}, bf16[2,36,16,128]{3,2,1,0:T(8,128)(2,1)S(1)}, u32[]{:S(2)}, u32[]{:S(2)}) collective-permute-start(bf16[2,36,16,128]{3,2,1,0:T(8,128)(2,1)S(1)} %get-tuple-element.25), channel_id=1, source_target_pairs={{0,1},{1,2},{2,3},{3,4},{4,5},{5,6},{6,7},{7,8},{8,9},{9,10},{10,1... | collective-permute-start | bytes 884744 | tf_op jit(solution)/shard_map/ppermute | solution.py:18
  24.3 0.0 collective-permute-done.halo
  24.3 5.8 %k3.1 = (bf16[6,26,16,640]{3,2,1,0:T(8,128)(2,1)S(1)}, bf16[6,26,16,640]{3,2,1,0:T(8,128)(2,1)S(1)}, bf16[6,26,16,640]{3,2,1,0:T(8,128)(2,1)S(1)}, bf16[2,2,24,1...) custom-call(s32[4]{0:T(128)S(1)} %copy-done.3, ...), custom_call_target="tpu_custom_call", output_to_operand_aliasing={{0}: (6, {}), {1}: (7, {})} | custom-call | flops 3057647616 | bytes 4194304 | tf_op jit(solution)/shard_map/k3/pallas_call | solution.py:416
  30.1 3.5 %collective-permute-start.2 = (bf16[2,36,16,128]{3,2,1,0:T(8,128)(2,1)S(1)}, bf16[2,36,16,128]{3,2,1,0:T(8,128)(2,1)S(1)}, u32[]{:S(2)}, u32[]{:S(2)}) collective-permute-start(bf16[2,36,16,128]{3,2,1,0:T(8,128)(2,1)S(1)} %get-tuple-element.24), channel_id=1, source_target_pairs={{0,1},{1,2},{2,3},{3,4},{4,5},{5,6},{6,7},{7,8},{8,9},{9,10},{10,1... | collective-permute-start | bytes 884744 | tf_op jit(solution)/shard_map/ppermute | solution.py:18
  33.6 0.0 collective-permute-done.3.halo
  33.6 5.3 %k4.1 = (bf16[6,26,16,640]{3,2,1,0:T(8,128)(2,1)S(1)}, bf16[6,26,16,640]{3,2,1,0:T(8,128)(2,1)S(1)}, bf16[2,16,4608]{2,1,0:T(8,128)(2,1)S(1)}) custom-call(s32[4]{0:T(128)S(1)} %copy-done.3, s32[4]{0:T(128)S(1)} %copy-done.4, bf16[2,36,16,128]{3,2,1,0:T(8,128)(2,1)S(1)} %collective-permute-done.3.halo, ...), custom_call_target="tpu_custom_call", output_to_operand_aliasing={{0}: (5, {}), {1}: (6, {})} | custom-call | flops 3057647616 | bytes 4194304 | tf_op jit(solution)/shard_map/k4/pallas_call | solution.py:427
  39.0 0.0 collective-permute-done.2.halo
  39.0 3.8 %k5.1 = (bf16[6,26,16,640]{3,2,1,0:T(8,128)(2,1)S(1)}, bf16[4,16,4608]{2,1,0:T(8,128)(2,1)}) custom-call(s32[4]{0:T(128)S(1)} %copy-done.3, s32[4]{0:T(128)S(1)} %copy-done.4, bf16[2,36,16,128]{3,2,1,0:T(8,128)(2,1)S(1)} %collective-permute-done.2.halo, bf16[4,27,192,192]{3,2,1,0:T(8,128)(2,1)S(1)} %bitcast.5, ...), custom_call_target="tpu_custom_call", output_to_operand_aliasing={{0}: (4, {})} | custom-call | flops 1528823808 | bytes 4194304 | tf_op jit(solution)/shard_map/k5/pallas_call | solution.py:436
Async XLA Ops:
  1.0 15.1 %collective-permute-start.1 = (bf16[2,16,4608]{2,1,0:T(8,128)(2,1)S(1)}, bf16[2,16,4608]{2,1,0:T(8,128)(2,1)S(1)}, u32[]{:S(2)}, u32[]{:S(2)}) collective-permute-start(bf16[2,16,4608]{2,1,0:T(8,128)(2,1)S(1)} %slice.3), channel_id=1, source_target_pairs={{0,1},{1,2},{2,3},{3,4},{4,5},{5,6},{6,7},{7,8},{8,9},{9,10},{10,1... | collective-permute-start | bytes 884744 | tf_op jit(solution)/shard_map/ppermute | solution.py:18
  3.4 12.7 %copy-start = (bf16[4,3,3,3,192,192]{5,4,3,2,1,0:T(8,128)(2,1)S(1)}, bf16[4,3,3,3,192,192]{5,4,3,2,1,0:T(8,128)(2,1)}, u32[]{:S(2)}) copy-start(bf16[4,3,3,3,192,192]{5,4,3,2,1,0:T(8,128)(2,1)} %param.7) | copy-start | bytes 23887876
  3.4 12.7 %copy-start.1 = (bf16[4,16,4608]{2,1,0:T(8,128)(2,1)S(1)}, bf16[4,16,4608]{2,1,0:T(8,128)(2,1)}, u32[]{:S(2)}) copy-start(bf16[4,16,4608]{2,1,0:T(8,128)(2,1)} %dense.3) | copy-start | bytes 1769476
  3.4 12.7 %copy-start.2 = (f32[4,192]{1,0:T(4,128)S(1)}, f32[4,192]{1,0:T(4,128)}, u32[]{:S(2)}) copy-start(f32[4,192]{1,0:T(4,128)} %gains.5) | copy-start | bytes 9220
  3.4 12.7 %copy-start.3 = (s32[4]{0:T(128)S(1)}, s32[4]{0:T(128)}, u32[]{:S(2)}) copy-start(s32[4]{0:T(128)} %starts.7) | copy-start | bytes 52
  3.5 12.7 %copy-start.4 = (s32[4]{0:T(128)S(1)}, s32[4]{0:T(128)}, u32[]{:S(2)}) copy-start(s32[4]{0:T(128)} %frames.7) | copy-start | bytes 52
  11.6 12.7 %collective-permute-start = (bf16[2,36,16,128]{3,2,1,0:T(8,128)(2,1)S(1)}, bf16[2,36,16,128]{3,2,1,0:T(8,128)(2,1)S(1)}, u32[]{:S(2)}, u32[]{:S(2)}) collective-permute-start(bf16[2,36,16,128]{3,2,1,0:T(8,128)(2,1)S(1)} %get-tuple-element.19), channel_id=1, source_target_pairs={{0,1},{1,2},{2,3},{3,4},{4,5},{5,6},{6,7},{7,8},{8,9},{9,10},{10,1... | collective-permute-start | bytes 884744 | tf_op jit(solution)/shard_map/ppermute | solution.py:18
  22.2 11.5 %collective-permute-start.3 = (bf16[2,36,16,128]{3,2,1,0:T(8,128)(2,1)S(1)}, bf16[2,36,16,128]{3,2,1,0:T(8,128)(2,1)S(1)}, u32[]{:S(2)}, u32[]{:S(2)}) collective-permute-start(bf16[2,36,16,128]{3,2,1,0:T(8,128)(2,1)S(1)} %get-tuple-element.25), channel_id=1, source_target_pairs={{0,1},{1,2},{2,3},{3,4},{4,5},{5,6},{6,7},{7,8},{8,9},{9,10},{10,1... | collective-permute-start | bytes 884744 | tf_op jit(solution)/shard_map/ppermute | solution.py:18
  30.1 8.9 %collective-permute-start.2 = (bf16[2,36,16,128]{3,2,1,0:T(8,128)(2,1)S(1)}, bf16[2,36,16,128]{3,2,1,0:T(8,128)(2,1)S(1)}, u32[]{:S(2)}, u32[]{:S(2)}) collective-permute-start(bf16[2,36,16,128]{3,2,1,0:T(8,128)(2,1)S(1)} %get-tuple-element.24), channel_id=1, source_target_pairs={{0,1},{1,2},{2,3},{3,4},{4,5},{5,6},{6,7},{7,8},{8,9},{9,10},{10,1... | collective-permute-start | bytes 884744 | tf_op jit(solution)/shard_map/ppermute | solution.py:18

commit v2 on v1

v2 whole, which is shorter than its diff:
```python
import jax
import jax.numpy as jnp
from jax import lax
from jax.experimental import pallas as pl
from jax.experimental.pallas import tpu as pltpu
from jax.sharding import PartitionSpec as P


LANES = 128
HALO = 2
STEP = 4
STAGED = 1
OLD_FIRST = (0, 1, 2)
NEW_FIRST = (2, 1, 0)
WHOLE = (1, 1)
LAST_SPLIT = (1, 1)
VMEM = pltpu.VMEM


def passed_along(value, axis, swap_first):
    count = lax.axis_size(axis)
    swap = [(i, i ^ 1) for i in range(count)]
    cross = [(i, i + 1) for i in range(1, count - 1, 2)]
    orders = {"a": swap, "b": cross} if swap_first else {"a": cross, "b": swap}
    results = []
    for pairs in orders.values():
        results.append(lax.ppermute(value, axis, pairs))
    return tuple(results) if swap_first else tuple(results[::-1])


def received(swapped, crossed, index):
    odd = lax.rem(lax.axis_index("tm"), 2) == 1
    return jnp.where(odd, swapped[index].astype(jnp.float32), crossed[index].astype(jnp.float32))


def low_half(shape):
    return lax.broadcasted_iota(jnp.int32, shape, len(shape) - 1) < LANES // 2


def swap_half(value):
    return pltpu.roll(value, LANES // 2, axis=value.ndim - 1)


def activate(main, rest, gain_main, gain_rest, channels):
    total = jnp.sum(main * main + rest * rest, axis=-1, keepdims=True)
    inverse = lax.rsqrt(total * (1.0 / channels) + 1e-06)

    def silu(value, gain):
        scaled = value * inverse * gain
        half = 0.5 * scaled
        return half * jnp.tanh(half) + half

    return silu(main, gain_main), silu(rest, gain_rest)


def load_gain(gain_pad, index):
    return gain_pad[index, 0][None, None, :], gain_pad[index, 1][None, None, :]


def fill_gain(gains, gain_pad):
    count, channels = gains.shape
    gain_pad[...] = jnp.zeros_like(gain_pad)
    for k in range(count):
        gain_pad[k, 0:1, :] = gains[k : k + 1, 0:LANES]
        gain_pad[k, 1:2, 0 : channels - LANES] = gains[k : k + 1, LANES:channels]


def dense_chunk(frame, chunk):
    width = STEP * 192
    return (frame, slice(None), slice(chunk * width, (chunk + 1) * width))


def unpack_dense(block):
    rows, width = block.shape
    block = block.astype(jnp.float32)
    tile = [block[:, LANES * i : LANES * (i + 1)] for i in range(width // LANES)]
    low = low_half((rows, LANES))
    main, rest = [], []
    for i in range(0, len(tile), 3):
        rolled_b, rolled_c = swap_half(tile[i + 1]), swap_half(tile[i + 2])
        main += [tile[i], jnp.where(low, rolled_b, rolled_c)]
        rest += [jnp.where(low, tile[i + 1], 0.0), jnp.where(low, rolled_c, 0.0)]
    return jnp.stack(main), jnp.stack(rest)


def pack_dense(target, frame, chunk, main, rest):
    rows = target.shape[1]
    width = STEP * 192
    low = low_half((rows, LANES))
    tile = []
    for i in range(0, STEP, 2):
        rolled = swap_half(main[i + 1])
        tile += [main[i], jnp.where(low, rest[i], rolled), jnp.where(low, rolled, swap_half(rest[i + 1]))]
    block = jnp.concatenate(tile, axis=-1).astype(target.dtype)
    target[frame, :, chunk * width : (chunk + 1) * width] = block


def unpack_wire(read, cols, frame, chunk):
    main = read((frame, pl.ds(STEP * chunk, STEP)))
    pair = read((frame, pl.ds(cols + STEP // 2 * chunk, STEP // 2)))
    low = low_half(pair.shape)
    rest = jnp.stack([jnp.where(low, pair, 0.0), jnp.where(low, swap_half(pair), 0.0)], axis=1)
    return main, rest.reshape(main.shape)


def pack_wire(target, frame, chunk, main, rest):
    cols = target.shape[1] * 2 // 3
    target[frame, pl.ds(STEP * chunk, STEP)] = main.astype(target.dtype)
    pair = rest.reshape((STEP // 2, 2) + rest.shape[1:])
    target[frame, pl.ds(cols + STEP // 2 * chunk, STEP // 2)] = (pair[:, 0] + swap_half(pair[:, 1])).astype(target.dtype)


def clear_borders(buf):
    frames, slots, rows, lanes = buf.shape
    for frame in range(frames):
        for slot in (0, slots - 2, slots - 1):
            buf[frame, slot] = jnp.zeros((rows, lanes), buf.dtype)


def store_pieces(buf, frame, chunk, main, rest):
    rows = main.shape[1]
    row = lax.broadcasted_iota(jnp.int32, main.shape, 1)

    def above(value):
        return jnp.where(row == 0, 0.0, pltpu.roll(value, 1, axis=1))

    def below(value):
        return jnp.where(row == rows - 1, 0.0, pltpu.roll(value, rows - 1, axis=1))

    def put(first_slot, lane, value):
        buf[frame, pl.ds(first_slot, STEP), :, lane : lane + value.shape[-1]] = value.astype(buf.dtype)

    slot = STEP * chunk + 1
    put(slot, 0, above(main))
    put(slot, LANES, main)
    put(slot, 2 * LANES, below(main))
    put(slot, 3 * LANES, above(rest) + swap_half(rest))
    lower = below(rest)
    put(slot, 4 * LANES, lower[..., : LANES // 2])
    put(slot - 1, 4 * LANES + LANES // 2, lower[..., : LANES // 2])


def convolve(buf, frame, weight, hidden, slot, first_col, cols, taps):
    rows = buf.shape[2]
    channels = weight.shape[-1]
    span = channels - LANES

    def piece(tap, col, lane):
        return buf[frame + tap, first_col + col : first_col + col + cols, :, lane : lane + LANES].reshape(cols * rows, LANES)

    def taken(tap, row, col, rest):
        index = (tap * 3 + row) * 3 + col
        return weight[index, LANES:channels, :] if rest else weight[index, 0:LANES, :]

    lhs, rhs = [], []
    for tap in taps:
        for col in range(3):
            for row in range(3):
                lhs.append(piece(tap, col, LANES * row))
                rhs.append(taken(tap, row, col, False))
            lhs.append(piece(tap, col, 3 * LANES))
            rhs += [taken(tap, 0, col, True), taken(tap, 1, col, True)]
        lhs.append(piece(tap, 0, 4 * LANES))
        rhs += [taken(tap, 2, 0, True), taken(tap, 2, 1, True)]
        lhs.append(piece(tap, 2, 4 * LANES))
        rhs += [taken(tap, 2, 2, True), jnp.zeros((span, channels), weight.dtype)]
    total = jnp.dot(jnp.concatenate(lhs, axis=1), jnp.concatenate(rhs, axis=0), preferred_element_type=jnp.float32)
    hidden[slot, 0, first_col : first_col + cols] = total[:, :LANES].reshape(cols, rows, LANES)
    hidden[slot, 1, first_col : first_col + cols, :, 0:span] = total[:, LANES:].reshape(cols, rows, span)


def each_chunk(cols, body):
    for chunk in range(cols // STEP):
        body(chunk)


def each_frame(count, body):
    for index in range(count):
        body(index)


def hidden_chunk(hidden, slot, chunk):
    return hidden[slot, 0, pl.ds(STEP * chunk, STEP)], hidden[slot, 1, pl.ds(STEP * chunk, STEP)]


def own_span(starts, frames):
    span = lax.axis_index("tm")
    own_start, own_frames = starts[0], frames[0]
    for v in range(1, starts.shape[0]):
        here = starts[v] <= span
        own_start = jnp.where(here, starts[v], own_start)
        own_frames = jnp.where(here, frames[v], own_frames)
    return span, own_start, own_frames


def keep_factor(starts, frames):
    span, own_start, _ = own_span(starts, frames)
    return jnp.where(span - 1 >= own_start, 1.0, 0.0).astype(jnp.float32)


def stage_kernel(dense_hbm, gains_hbm, weight_hbm, first, wire, dense, weight, gains, gain_pad, sems):
    copies = [
        pltpu.make_async_copy(dense_hbm, dense, sems.at[0]),
        pltpu.make_async_copy(gains_hbm, gains, sems.at[1]),
        pltpu.make_async_copy(dense_hbm.at[pl.ds(HALO, HALO)], wire, sems.at[2]),
        pltpu.make_async_copy(weight_hbm.at[pl.ds(0, 1)], weight, sems.at[3]),
    ]
    for copy in copies:
        copy.start()
    clear_borders(first)
    for copy in copies[:3]:
        copy.wait()
    fill_gain(gains, gain_pad)
    for frame in range(STAGED):
        dense_in(dense, first, frame, gains, gain_pad)
    copies[3].wait()


def dense_in(dense, first, frame, gains, gain_pad):
    channels = gains.shape[1]

    def body(chunk):
        main, rest = unpack_dense(dense[dense_chunk(frame, chunk)])
        main, rest = activate(main, rest, *load_gain(gain_pad, 0), channels)
        store_pieces(first, frame + HALO, chunk, main, rest)

    each_chunk(first.shape[1] - 2, body)


def first_kernel(dense, gains, weight, weight_hbm, first_in, first, wire, later_weight, hidden, gain_pad, sem):
    copy = pltpu.make_async_copy(weight_hbm.at[pl.ds(1, later_weight.shape[0])], later_weight, sem)
    copy.start()
    fill_gain(gains, gain_pad)
    hidden[:, 1] = jnp.zeros_like(hidden[:, 1])
    for frame in range(STAGED, dense.shape[0]):
        dense_in(dense, first, frame, gains, gain_pad)
    hidden_out(first, HALO, weight.at[0], 0, hidden, gains, gain_pad, 1, None, wire, OLD_FIRST, LAST_SPLIT)
    copy.wait()


def convolve_frames(source, base, weight, layer, hidden, taps, splits, finish):
    cols = source.shape[1] - 2
    for i in range(HALO):
        part = cols // splits[i]
        for first_col in range(0, cols, part):
            slot = 2 * (layer % 2) + i
            convolve(source, base + i, weight, hidden, slot, first_col, part, taps)
            for chunk in range(first_col // STEP, (first_col + part) // STEP):
                finish(i, chunk, *hidden_chunk(hidden, slot, chunk))


def hidden_out(source, base, weight, layer, hidden, gains, gain_pad, gain_index, target, wire, taps, splits):
    channels = gains.shape[1]

    def finish(i, chunk, main, rest):
        main, rest = activate(main, rest, *load_gain(gain_pad, gain_index), channels)
        if wire is None:
            store_pieces(target, base + HALO + i, chunk, main, rest)
        else:
            pack_wire(wire, i, chunk, main, rest)

    convolve_frames(source, base, weight, layer, hidden, taps, splits, finish)


def residual_out(source, base, weight, layer, hidden, taps, splits, finish):
    convolve_frames(source, base, weight, layer, hidden, taps, splits, finish)


def rounded(value):
    return value.astype(jnp.bfloat16).astype(jnp.float32)


def state_put(state, i, chunk, main, rest):
    state[i, 0, pl.ds(STEP * chunk, STEP)] = main.astype(state.dtype)
    state[i, 1, pl.ds(STEP * chunk, STEP)] = rest.astype(state.dtype)


def state_get(state, i, chunk):
    return (
        state[i, 0, pl.ds(STEP * chunk, STEP)].astype(jnp.float32),
        state[i, 1, pl.ds(STEP * chunk, STEP)].astype(jnp.float32),
    )


def wire_in(read, target, base):
    cols = target.shape[1] - 2
    for frame in range(HALO):
        each_chunk(cols, lambda chunk: store_pieces(target, base + frame, chunk, *unpack_wire(read, cols, frame, chunk)))


def halo_in(swapped, crossed, target, keep):
    wire_in(lambda index: received(swapped, crossed, index) * keep, target, 0)


def own_in(wire, target):
    wire_in(lambda index: wire[index].astype(jnp.float32), target, 2 * HALO)


def second_kernel(
    starts, frames, swapped, crossed, dense, gains, own, weight, later_weight, first_in, first, second, state, wire, hidden, gain_pad
):
    cols = first.shape[1] - 2
    channels = gains.shape[1]
    keep = keep_factor(starts, frames)
    fill_gain(gains, gain_pad)
    clear_borders(second)
    own_in(own, second)
    hidden[:, 1] = jnp.zeros_like(hidden[:, 1])

    def enter(frame):
        def body(chunk):
            main, rest = unpack_dense(received(swapped, crossed, dense_chunk(frame, chunk)))
            main, rest = activate(main, rest, *load_gain(gain_pad, 0), channels)
            store_pieces(first, frame, chunk, main * keep, rest * keep)

        each_chunk(cols, body)

    each_frame(HALO, enter)
    hidden_out(first, 0, weight.at[0], 0, hidden, gains, gain_pad, 1, second, None, NEW_FIRST, WHOLE)

    def finish(i, chunk, main, rest):
        main_in, rest_in = unpack_dense(dense[dense_chunk(HALO + i, chunk)])
        main, rest = rounded(main + main_in), rounded(rest + rest_in)
        state_put(state, i, chunk, main, rest)
        main, rest = activate(main, rest, *load_gain(gain_pad, 2), channels)
        pack_wire(wire, i, chunk, main, rest)

    residual_out(second, HALO, later_weight.at[0], 1, hidden, NEW_FIRST, LAST_SPLIT, finish)


def third_kernel(
    starts, frames, swapped, crossed, dense, gains, own, later_weight, second_in, second, third, state, wire, hidden, gain_pad
):
    channels = gains.shape[1]
    keep = keep_factor(starts, frames)
    fill_gain(gains, gain_pad)
    clear_borders(third)
    own_in(own, third)
    hidden[:, 1] = jnp.zeros_like(hidden[:, 1])
    halo_in(swapped, crossed, second, keep)

    def finish(i, chunk, main, rest):
        main_in, rest_in = unpack_dense(dense[dense_chunk(i, chunk)])
        main, rest = rounded(main + main_in), rounded(rest + rest_in)
        state_put(state, i, chunk, main, rest)
        main, rest = activate(main, rest, *load_gain(gain_pad, 2), channels)
        store_pieces(third, HALO + i, chunk, main, rest)

    residual_out(second, 0, later_weight.at[0], 1, hidden, NEW_FIRST, WHOLE, finish)
    hidden_out(third, HALO, later_weight.at[1], 2, hidden, gains, gain_pad, 3, None, wire, NEW_FIRST, LAST_SPLIT)


def live_factor(starts, frames, frame, span_frames):
    span, own_start, own_frames = own_span(starts, frames)
    return jnp.where((span - own_start) * span_frames + frame < own_frames, 1.0, 0.0).astype(jnp.float32)


def fourth_kernel(
    starts, frames, swapped, crossed, gains, own, later_weight, third_in, state, third, fourth, out, hidden, gain_pad
):
    keep = keep_factor(starts, frames)
    fill_gain(gains, gain_pad)
    clear_borders(fourth)
    own_in(own, fourth)
    hidden[:, 1] = jnp.zeros_like(hidden[:, 1])
    halo_in(swapped, crossed, third, keep)
    hidden_out(third, 0, later_weight.at[1], 2, hidden, gains, gain_pad, 3, fourth, None, NEW_FIRST, WHOLE)

    def finish(i, chunk, main, rest):
        main_in, rest_in = state_get(state, i, chunk)
        live = live_factor(starts, frames, HALO + i, 2 * HALO)
        pack_dense(out, i, chunk, (main + main_in) * live, (rest + rest_in) * live)

    residual_out(fourth, HALO, later_weight.at[2], 3, hidden, NEW_FIRST, LAST_SPLIT, finish)


def fifth_kernel(
    starts, frames, swapped, crossed, later_weight, fourth_in, state, later, fourth, out, hidden, stage, sems
):
    keep = keep_factor(starts, frames)
    copies = [pltpu.make_async_copy(later, out.at[pl.ds(HALO, HALO)], sems.at[0])]
    copies[0].start()
    hidden[:, 1] = jnp.zeros_like(hidden[:, 1])
    halo_in(swapped, crossed, fourth, keep)

    def finish(i, chunk, main, rest):
        main_in, rest_in = state_get(state, i, chunk)
        live = live_factor(starts, frames, i, 2 * HALO)
        pack_dense(stage, i, chunk, (main + main_in) * live, (rest + rest_in) * live)

    residual_out(fourth, 0, later_weight.at[2], 3, hidden, NEW_FIRST, LAST_SPLIT, finish)
    for i in range(HALO):
        copies.append(pltpu.make_async_copy(stage.at[i], out.at[i], sems.at[1 + i]))
        copies[-1].start()
    for copy in copies:
        copy.wait()


def local(features, gains, conv_weights, video_frames, video_start):
    frames, rows, merged = features.shape
    channels = gains.shape[1]
    cols = merged // channels
    layers = conv_weights.shape[0]
    weight = conv_weights.reshape(layers, 27, channels, channels)
    bf16, f32 = jnp.bfloat16, jnp.float32
    pieces = jax.ShapeDtypeStruct((frames + HALO, cols + 2, rows, 5 * LANES), bf16)
    wire = jax.ShapeDtypeStruct((HALO, cols * 3 // 2, rows, LANES), bf16)
    state = jax.ShapeDtypeStruct((HALO, 2, cols, rows, LANES), bf16)
    hidden = VMEM((2 * HALO, 2, cols, rows, LANES), f32)
    gain_pad = VMEM((layers, 2, LANES), f32)
    smem = pl.BlockSpec(memory_space=pltpu.SMEM)
    vmem = pl.BlockSpec(memory_space=VMEM)
    hbm = pl.BlockSpec(memory_space=pltpu.HBM)

    def call(body, ins, outs, scratch, convs, aliases=None, out_specs=None):
        return pl.pallas_call(
            body,
            out_shape=outs,
            in_specs=ins,
            out_specs=out_specs or tuple(vmem for _ in outs),
            scratch_shapes=scratch,
            input_output_aliases=aliases or {},
            compiler_params=pltpu.CompilerParams(vmem_limit_bytes=12 << 20),
            cost_estimate=pl.CostEstimate(
                flops=convs * 2 * 27 * channels * channels * rows * cols * 2,
                bytes_accessed=4 << 20,
                transcendentals=0,
            ),
        )

    def weights(count):
        return jax.ShapeDtypeStruct((count, 27, channels, channels), bf16)

    dense = jax.ShapeDtypeStruct(features.shape, bf16)
    dense_half = jax.ShapeDtypeStruct((HALO, rows, merged), bf16)
    dma = pltpu.SemaphoreType.DMA
    features_hbm, gains_hbm, weight_hbm = (
        pltpu.with_memory_space_constraint(a, pltpu.HBM) for a in (features, gains, weight)
    )
    scalars = (video_start, video_frames)

    first, wire0, features, weight0 = call(
        stage_kernel,
        [hbm, hbm, hbm],
        (pieces, dense_half, dense, weights(1)),
        [VMEM(gains.shape, f32), gain_pad, dma((4,))],
        0,
    )(features_hbm, gains_hbm, weight_hbm)
    halo0 = passed_along(wire0, "tm", True)
    first, wire1, later_weight = call(
        first_kernel,
        [vmem, vmem, vmem, hbm, vmem],
        (pieces, wire, weights(layers - 1)),
        [hidden, gain_pad, dma],
        1,
        {4: 0},
    )(features, gains, weight0, weight_hbm, first)
    halo1 = passed_along(wire1, "tm", False)
    _, second, state_late, wire2 = call(
        second_kernel, [smem, smem] + [vmem] * 8, (pieces, pieces, state, wire), [hidden, gain_pad], 2, {9: 0}
    )(*scalars, *halo0, features, gains, wire1, weight0, later_weight, first)
    halo2 = passed_along(wire2, "tm", True)
    _, third, state_early, wire3 = call(
        third_kernel, [smem, smem] + [vmem] * 7, (pieces, pieces, state, wire), [hidden, gain_pad], 2, {8: 0}
    )(*scalars, *halo1, features, gains, wire2, later_weight, second)
    halo3 = passed_along(wire3, "tm", False)
    _, fourth, later = call(
        fourth_kernel, [smem, smem] + [vmem] * 7, (pieces, pieces, dense_half), [hidden, gain_pad], 2, {7: 0}
    )(*scalars, *halo2, gains, wire3, later_weight, third, state_late)
    _, out = call(
        fifth_kernel,
        [smem, smem] + [vmem] * 6,
        (pieces, dense),
        [hidden, VMEM(dense_half.shape, bf16), dma((1 + HALO,))],
        1,
        {5: 0},
        (vmem, hbm),
    )(*scalars, *halo3, later_weight, fourth, state_early, later)
    return out


def solution(mesh):
    in_specs = (P(("grp", "tm"), None, None), P(), P(), P("grp"), P("grp"))
    out_specs = P(("grp", "tm"), None, None)
    return jax.shard_map(local, mesh=mesh, in_specs=in_specs, out_specs=out_specs, check_vma=False)
```

time: 43 us -> 42.2 us (0.981)
  the two profiles are of different devices: /device:TPU:0 before, /device:TPU:1 now
where the time goes in v2:
time: 42.2 us; the launch traced here: 42 us
  Pallas kernels  26 us (62%)
  starting transfers between devices  15.6 us (37%)
    ppermute x8, starting transfers between devices, passed_along(): results.append(lax.ppermute(value, axis, pairs))  15.6 us
    pallas_call x1, Pallas kernels, local(): call(second_kernel, [smem, smem] + [vmem] * 8, (pieces, pieces, state, wi...  5.75 us
    pallas_call x1, Pallas kernels, local(): call(third_kernel, [smem, smem] + [vmem] * 7, (pieces, pieces, state, wir...  5.71 us
    pallas_call x1, Pallas kernels, local(): call(fourth_kernel, [smem, smem] + [vmem] * 7, (pieces, pieces, dense_hal...  5.48 us
    pallas_call x1, Pallas kernels, local(): call(fifth_kernel, [smem, smem] + [vmem] * 6, (pieces, dense), [hidden, V...  3.69 us
    pallas_call x1, Pallas kernels, local(): call(first_kernel, [vmem, vmem, vmem, hbm, vmem], (pieces, wire, weights(...  3.28 us
    pallas_call x1, Pallas kernels, local(): call(stage_kernel, [hbm, hbm, hbm], (pieces, dense_half, dense, weights(1...  2.09 us
  transfers between devices with their start and end apart: 8, of which 0 were waited for; matrix products, arithmetic and copies ran while one was open for 0% of the time, Pallas kernels for 48%

profile of v2, /device:TPU:1, one launch (start us, length us, event | category | flops | bytes accessed | tf_op | source)
XLA Modules:
  0.0 42.0 jit_solution(4547804044477564950)
XLA Ops:
  0.0 0.0 copy-start
  0.0 2.1 %shard_map.55 = (bf16[6,26,16,640]{3,2,1,0:T(8,128)(2,1)S(1)}, bf16[2,16,4608]{2,1,0:T(8,128)(2,1)S(1)}, bf16[4,16,4608]{2,1,0:T(8,128)(2,1)S(1)}, bf16[1,27,192,192]{3,2,1,0:T(8,128)(2,1)S(1)}) custom-call(bf16[4,16,4608]{2,1,0:T(8,128)(2,1)} %dense_hbm.1, f32[4,192]{1,0:T(4,128)} %gains.7, bf16[4,27,192,192]{3,2,1,0:T(8,128)(2,1)} %bitcast.1), custom_call_target="tpu_custom_call" | custom-call | bytes 4194304 | tf_op jit(solution)/shard_map/pallas_call | solution.py:442
  2.1 0.1 collective-permute-start.2
  2.2 4.5 %collective-permute-start.3 = (bf16[2,16,4608]{2,1,0:T(8,128)(2,1)S(1)}, bf16[2,16,4608]{2,1,0:T(8,128)(2,1)S(1)}, u32[]{:S(2)}, u32[]{:S(2)}) collective-permute-start(bf16[2,16,4608]{2,1,0:T(8,128)(2,1)S(1)} %get-tuple-element.25), channel_id=1, source_target_pairs={{1,2},{3,4},{5,6},{7,8},{9,10},{11,12},{13,14},{17,18},{19,20},{21... | collective-permute-start | bytes 884744 | tf_op jit(solution)/shard_map/ppermute | solution.py:27
  6.7 0.0 copy-done
  6.7 0.0 copy-start.1
  6.8 0.0 copy-start.2
  6.8 3.3 %shard_map.56 = (bf16[6,26,16,640]{3,2,1,0:T(8,128)(2,1)S(1)}, bf16[2,36,16,128]{3,2,1,0:T(8,128)(2,1)S(1)}, bf16[3,27,192,192]{3,2,1,0:T(8,128)(2,1)S(1)}) custom-call(bf16[4,16,4608]{2,1,0:T(8,128)(2,1)S(1)} %get-tuple-element.21.dense, f32[4,192]{1,0:T(4,128)S(1)} %copy-done, ...), custom_call_target="tpu_custom_call", output_to_operand_aliasing={{0}: (4, {})} | custom-call | flops 1528823808 | bytes 4194304 | tf_op jit(solution)/shard_map/pallas_call | solution.py:450
  10.1 0.1 collective-permute-start
  10.1 3.5 %collective-permute-start.1 = (bf16[2,36,16,128]{3,2,1,0:T(8,128)(2,1)S(1)}, bf16[2,36,16,128]{3,2,1,0:T(8,128)(2,1)S(1)}, u32[]{:S(2)}, u32[]{:S(2)}) collective-permute-start(bf16[2,36,16,128]{3,2,1,0:T(8,128)(2,1)S(1)} %get-tuple-element.24.own), channel_id=1, source_target_pairs={{1,2},{3,4},{5,6},{7,8},{9,10},{11,12},{13,14},{17,18},{19,20},{21... | collective-permute-start | bytes 884744 | tf_op jit(solution)/shard_map/ppermute | solution.py:27
  13.7 0.0 collective-permute-done.2.swapped
  13.7 0.0 collective-permute-done.3.crossed
  13.7 0.0 copy-done.1
  13.7 0.0 copy-done.2
  13.7 5.7 %shard_map.57 = (bf16[6,26,16,640]{3,2,1,0:T(8,128)(2,1)S(1)}, bf16[6,26,16,640]{3,2,1,0:T(8,128)(2,1)S(1)}, bf16[2,2,24,16,128]{4,3,2,1,0:T(8,128)(2,1)S(1)}, bf16[2,36,16,128]{3,2,1,0:T(8,128)(2,1)S(1)}) custom-call(s32[4]{0:T(128)S(1)} %copy-done.1, s32[4]{0:T(128)S(1)} %copy-done.2, ...), custom_call_target="tpu_custom_call", output_to_operand_aliasing={{0}: (9, {})} | custom-call | flops 3057647616 | bytes 4194304 | tf_op jit(solution)/shard_map/pallas_call | solution.py:459
  19.5 0.1 collective-permute-start.6
  19.5 3.7 %collective-permute-start.7 = (bf16[2,36,16,128]{3,2,1,0:T(8,128)(2,1)S(1)}, bf16[2,36,16,128]{3,2,1,0:T(8,128)(2,1)S(1)}, u32[]{:S(2)}, u32[]{:S(2)}) collective-permute-start(bf16[2,36,16,128]{3,2,1,0:T(8,128)(2,1)S(1)} %get-tuple-element.28.own), channel_id=1, source_target_pairs={{1,2},{3,4},{5,6},{7,8},{9,10},{11,12},{13,14},{17,18},{19,20},{21... | collective-permute-start | bytes 884744 | tf_op jit(solution)/shard_map/ppermute | solution.py:27
  23.3 0.0 collective-permute-done.swapped
  23.3 0.0 collective-permute-done.1.crossed
  23.3 5.7 %shard_map.58 = (bf16[6,26,16,640]{3,2,1,0:T(8,128)(2,1)S(1)}, bf16[6,26,16,640]{3,2,1,0:T(8,128)(2,1)S(1)}, bf16[2,2,24,16,128]{4,3,2,1,0:T(8,128)(2,1)S(1)}, bf16[2,36,16,128]{3,2,1,0:T(8,128)(2,1)S(1)}) custom-call(s32[4]{0:T(128)S(1)} %copy-done.1, s32[4]{0:T(128)S(1)} %copy-done.2, ...), custom_call_target="tpu_custom_call", output_to_operand_aliasing={{0}: (8, {})} | custom-call | flops 3057647616 | bytes 4194304 | tf_op jit(solution)/shard_map/pallas_call | solution.py:463
  29.0 0.1 collective-permute-start.4
  29.1 3.5 %collective-permute-start.5 = (bf16[2,36,16,128]{3,2,1,0:T(8,128)(2,1)S(1)}, bf16[2,36,16,128]{3,2,1,0:T(8,128)(2,1)S(1)}, u32[]{:S(2)}, u32[]{:S(2)}) collective-permute-start(bf16[2,36,16,128]{3,2,1,0:T(8,128)(2,1)S(1)} %get-tuple-element.30.own), channel_id=1, source_target_pairs={{1,2},{3,4},{5,6},{7,8},{9,10},{11,12},{13,14},{17,18},{19,20},{21... | collective-permute-start | bytes 884744 | tf_op jit(solution)/shard_map/ppermute | solution.py:27
  32.6 0.0 collective-permute-done.6.swapped
  32.6 0.0 collective-permute-done.7.crossed
  32.6 5.5 %shard_map.59 = (bf16[6,26,16,640]{3,2,1,0:T(8,128)(2,1)S(1)}, bf16[6,26,16,640]{3,2,1,0:T(8,128)(2,1)S(1)}, bf16[2,16,4608]{2,1,0:T(8,128)(2,1)S(1)}) custom-call(s32[4]{0:T(128)S(1)} %copy-done.1, s32[4]{0:T(128)S(1)} %copy-done.2, bf16[2,36,16,128]{3,2,1,0:T(8,128)(2,1)S(1)} %collective-permute-done.6.swapped, ...), custom_call_target="tpu_custom_call", output_to_operand_aliasing={{0}: (7, {})} | custom-call | flops 3057647616 | bytes 4194304 | tf_op jit(solution)/shard_map/pallas_call | solution.py:467
  38.1 0.0 collective-permute-done.4.swapped
  38.1 0.0 collective-permute-done.5.crossed
  38.1 3.7 %shard_map.60 = (bf16[6,26,16,640]{3,2,1,0:T(8,128)(2,1)S(1)}, bf16[4,16,4608]{2,1,0:T(8,128)(2,1)}) custom-call(s32[4]{0:T(128)S(1)} %copy-done.1, s32[4]{0:T(128)S(1)} %copy-done.2, bf16[2,36,16,128]{3,2,1,0:T(8,128)(2,1)S(1)} %collective-permute-done.4.swapped, ...), custom_call_target="tpu_custom_call", output_to_operand_aliasing={{0}: (5, {})} | custom-call | flops 1528823808 | bytes 4194304 | tf_op jit(solution)/shard_map/pallas_call | solution.py:470
Async XLA Ops:
  0.0 6.7 %copy-start = (f32[4,192]{1,0:T(4,128)S(1)}, f32[4,192]{1,0:T(4,128)}, u32[]{:S(2)}) copy-start(f32[4,192]{1,0:T(4,128)} %gains.7) | copy-start | bytes 9220
  2.1 11.6 %collective-permute-start.2 = (bf16[2,16,4608]{2,1,0:T(8,128)(2,1)S(1)}, bf16[2,16,4608]{2,1,0:T(8,128)(2,1)S(1)}, u32[]{:S(2)}, u32[]{:S(2)}) collective-permute-start(bf16[2,16,4608]{2,1,0:T(8,128)(2,1)S(1)} %get-tuple-element.25), channel_id=1, source_target_pairs={{0,1},{1,0},{2,3},{3,2},{4,5},{5,4},{6,7},{7,6},{8,9},{9,8},{10,11... | collective-permute-start | bytes 884744 | tf_op jit(solution)/shard_map/ppermute | solution.py:27
  2.2 11.5 %collective-permute-start.3 = (bf16[2,16,4608]{2,1,0:T(8,128)(2,1)S(1)}, bf16[2,16,4608]{2,1,0:T(8,128)(2,1)S(1)}, u32[]{:S(2)}, u32[]{:S(2)}) collective-permute-start(bf16[2,16,4608]{2,1,0:T(8,128)(2,1)S(1)} %get-tuple-element.25), channel_id=1, source_target_pairs={{1,2},{3,4},{5,6},{7,8},{9,10},{11,12},{13,14},{17,18},{19,20},{21... | collective-permute-start | bytes 884744 | tf_op jit(solution)/shard_map/ppermute | solution.py:27
  6.7 7.0 %copy-start.1 = (s32[4]{0:T(128)S(1)}, s32[4]{0:T(128)}, u32[]{:S(2)}) copy-start(s32[4]{0:T(128)} %starts.7) | copy-start | bytes 52
  6.8 7.0 %copy-start.2 = (s32[4]{0:T(128)S(1)}, s32[4]{0:T(128)}, u32[]{:S(2)}) copy-start(s32[4]{0:T(128)} %frames.7) | copy-start | bytes 52
  10.1 13.2 %collective-permute-start = (bf16[2,36,16,128]{3,2,1,0:T(8,128)(2,1)S(1)}, bf16[2,36,16,128]{3,2,1,0:T(8,128)(2,1)S(1)}, u32[]{:S(2)}, u32[]{:S(2)}) collective-permute-start(bf16[2,36,16,128]{3,2,1,0:T(8,128)(2,1)S(1)} %get-tuple-element.24.own), channel_id=1, source_target_pairs={{0,1},{1,0},{2,3},{3,2},{4,5},{5,4},{6,7},{7,6},{8,9},{9,8},{10,11... | collective-permute-start | bytes 884744 | tf_op jit(solution)/shard_map/ppermute | solution.py:27
  10.1 13.1 %collective-permute-start.1 = (bf16[2,36,16,128]{3,2,1,0:T(8,128)(2,1)S(1)}, bf16[2,36,16,128]{3,2,1,0:T(8,128)(2,1)S(1)}, u32[]{:S(2)}, u32[]{:S(2)}) collective-permute-start(bf16[2,36,16,128]{3,2,1,0:T(8,128)(2,1)S(1)} %get-tuple-element.24.own), channel_id=1, source_target_pairs={{1,2},{3,4},{5,6},{7,8},{9,10},{11,12},{13,14},{17,18},{19,20},{21... | collective-permute-start | bytes 884744 | tf_op jit(solution)/shard_map/ppermute | solution.py:27
  19.5 13.2 %collective-permute-start.6 = (bf16[2,36,16,128]{3,2,1,0:T(8,128)(2,1)S(1)}, bf16[2,36,16,128]{3,2,1,0:T(8,128)(2,1)S(1)}, u32[]{:S(2)}, u32[]{:S(2)}) collective-permute-start(bf16[2,36,16,128]{3,2,1,0:T(8,128)(2,1)S(1)} %get-tuple-element.28.own), channel_id=1, source_target_pairs={{0,1},{1,0},{2,3},{3,2},{4,5},{5,4},{6,7},{7,6},{8,9},{9,8},{10,11... | collective-permute-start | bytes 884744 | tf_op jit(solution)/shard_map/ppermute | solution.py:27
  19.5 13.1 %collective-permute-start.7 = (bf16[2,36,16,128]{3,2,1,0:T(8,128)(2,1)S(1)}, bf16[2,36,16,128]{3,2,1,0:T(8,128)(2,1)S(1)}, u32[]{:S(2)}, u32[]{:S(2)}) collective-permute-start(bf16[2,36,16,128]{3,2,1,0:T(8,128)(2,1)S(1)} %get-tuple-element.28.own), channel_id=1, source_target_pairs={{1,2},{3,4},{5,6},{7,8},{9,10},{11,12},{13,14},{17,18},{19,20},{21... | collective-permute-start | bytes 884744 | tf_op jit(solution)/shard_map/ppermute | solution.py:27
  29.0 9.1 %collective-permute-start.4 = (bf16[2,36,16,128]{3,2,1,0:T(8,128)(2,1)S(1)}, bf16[2,36,16,128]{3,2,1,0:T(8,128)(2,1)S(1)}, u32[]{:S(2)}, u32[]{:S(2)}) collective-permute-start(bf16[2,36,16,128]{3,2,1,0:T(8,128)(2,1)S(1)} %get-tuple-element.30.own), channel_id=1, source_target_pairs={{0,1},{1,0},{2,3},{3,2},{4,5},{5,4},{6,7},{7,6},{8,9},{9,8},{10,11... | collective-permute-start | bytes 884744 | tf_op jit(solution)/shard_map/ppermute | solution.py:27
  29.1 9.1 %collective-permute-start.5 = (bf16[2,36,16,128]{3,2,1,0:T(8,128)(2,1)S(1)}, bf16[2,36,16,128]{3,2,1,0:T(8,128)(2,1)S(1)}, u32[]{:S(2)}, u32[]{:S(2)}) collective-permute-start(bf16[2,36,16,128]{3,2,1,0:T(8,128)(2,1)S(1)} %get-tuple-element.30.own), channel_id=1, source_target_pairs={{1,2},{3,4},{5,6},{7,8},{9,10},{11,12},{13,14},{17,18},{19,20},{21... | collective-permute-start | bytes 884744 | tf_op jit(solution)/shard_map/ppermute | solution.py:27

commit v3 on v2

--- a/solution.py
+++ b/solution.py
@@ -17,20 +17,26 @@
 VMEM = pltpu.VMEM
 
 
-def passed_along(value, axis, swap_first):
-    count = lax.axis_size(axis)
-    swap = [(i, i ^ 1) for i in range(count)]
-    cross = [(i, i + 1) for i in range(1, count - 1, 2)]
-    orders = {"a": swap, "b": cross} if swap_first else {"a": cross, "b": swap}
-    results = []
-    for pairs in orders.values():
-        results.append(lax.ppermute(value, axis, pairs))
-    return tuple(results) if swap_first else tuple(results[::-1])
-
-
-def received(swapped, crossed, index):
-    odd = lax.rem(lax.axis_index("tm"), 2) == 1
-    return jnp.where(odd, swapped[index].astype(jnp.float32), crossed[index].astype(jnp.float32))
+def is_odd():
+    return lax.rem(lax.axis_index("tm"), 2) == 1
+
+
+def plain(ref):
+    return lambda index: ref[index].astype(jnp.float32)
+
+
+def by_place(even_ref, odd_ref):
+    odd = is_odd()
+    return lambda index: jnp.where(odd, odd_ref[index].astype(jnp.float32), even_ref[index].astype(jnp.float32))
+
+
+def at_place(body, odd, inputs, carried):
+    def kernel(*refs):
+        @pl.when(is_odd() == odd)
+        def _():
+            body(*refs[:inputs], *refs[inputs + carried :])
+
+    return kernel
 
 
 def low_half(shape):
@@ -193,32 +199,35 @@
     return span, own_start, own_frames
 
 
-def keep_factor(starts, frames):
-    span, own_start, _ = own_span(starts, frames)
-    return jnp.where(span - 1 >= own_start, 1.0, 0.0).astype(jnp.float32)
-
-
-def stage_kernel(dense_hbm, gains_hbm, weight_hbm, first, wire, dense, weight, gains, gain_pad, sems):
+def stage_kernel(
+    dense_hbm, gains_hbm, weight_hbm, starts_hbm, frames_hbm, first, wire, dense, weight, gain_pad, facts, gains, starts, frames, sems
+):
     copies = [
         pltpu.make_async_copy(dense_hbm, dense, sems.at[0]),
         pltpu.make_async_copy(gains_hbm, gains, sems.at[1]),
         pltpu.make_async_copy(dense_hbm.at[pl.ds(HALO, HALO)], wire, sems.at[2]),
-        pltpu.make_async_copy(weight_hbm.at[pl.ds(0, 1)], weight, sems.at[3]),
+        pltpu.make_async_copy(starts_hbm, starts, sems.at[3]),
+        pltpu.make_async_copy(frames_hbm, frames, sems.at[4]),
+        pltpu.make_async_copy(weight_hbm.at[pl.ds(0, 1)], weight, sems.at[5]),
     ]
     for copy in copies:
         copy.start()
     clear_borders(first)
-    for copy in copies[:3]:
+    for copy in copies[:5]:
         copy.wait()
     fill_gain(gains, gain_pad)
+    span, own_start, own_frames = own_span(starts, frames)
+    factors = [jnp.where(span - 1 >= own_start, 1.0, 0.0)]
+    for frame in range(2 * HALO):
+        factors.append(jnp.where((span - own_start) * (2 * HALO) + frame < own_frames, 1.0, 0.0))
+    for row, factor in enumerate(factors):
+        facts[row] = jnp.full((LANES,), factor, facts.dtype)
     for frame in range(STAGED):
-        dense_in(dense, first, frame, gains, gain_pad)
-    copies[3].wait()
-
-
-def dense_in(dense, first, frame, gains, gain_pad):
-    channels = gains.shape[1]
-
+        dense_in(dense, first, frame, gain_pad, gains.shape[1])
+    copies[5].wait()
+
+
+def dense_in(dense, first, frame, gain_pad, channels):
     def body(chunk):
         main, rest = unpack_dense(dense[dense_chunk(frame, chunk)])
         main, rest = activate(main, rest, *load_gain(gain_pad, 0), channels)
@@ -227,14 +236,13 @@
     each_chunk(first.shape[1] - 2, body)
 
 
-def first_kernel(dense, gains, weight, weight_hbm, first_in, first, wire, later_weight, hidden, gain_pad, sem):
+def first_kernel(dense, gain_pad, weight, weight_hbm, first, wire, later_weight, hidden, sem):
     copy = pltpu.make_async_copy(weight_hbm.at[pl.ds(1, later_weight.shape[0])], later_weight, sem)
     copy.start()
-    fill_gain(gains, gain_pad)
     hidden[:, 1] = jnp.zeros_like(hidden[:, 1])
     for frame in range(STAGED, dense.shape[0]):
-        dense_in(dense, first, frame, gains, gain_pad)
-    hidden_out(first, HALO, weight.at[0], 0, hidden, gains, gain_pad, 1, None, wire, OLD_FIRST, LAST_SPLIT)
+        dense_in(dense, first, frame, gain_pad, weight.shape[-1])
+    hidden_out(first, HALO, weight.at[0], 0, hidden, gain_pad, 1, None, wire, OLD_FIRST, LAST_SPLIT)
     copy.wait()
 
 
@@ -249,8 +257,8 @@
                 finish(i, chunk, *hidden_chunk(hidden, slot, chunk))
 
 
-def hidden_out(source, base, weight, layer, hidden, gains, gain_pad, gain_index, target, wire, taps, splits):
-    channels = gains.shape[1]
+def hidden_out(source, base, weight, layer, hidden, gain_pad, gain_index, target, wire, taps, splits):
+    channels = weight.shape[-1]
 
     def finish(i, chunk, main, rest):
         main, rest = activate(main, rest, *load_gain(gain_pad, gain_index), channels)
@@ -288,35 +296,34 @@
         each_chunk(cols, lambda chunk: store_pieces(target, base + frame, chunk, *unpack_wire(read, cols, frame, chunk)))
 
 
-def halo_in(swapped, crossed, target, keep):
-    wire_in(lambda index: received(swapped, crossed, index) * keep, target, 0)
-
-
-def own_in(wire, target):
-    wire_in(lambda index: wire[index].astype(jnp.float32), target, 2 * HALO)
+def halo_in(read, target, keep):
+    wire_in(lambda index: read(index) * keep, target, 0)
+
+
+def own_in(read, target):
+    wire_in(read, target, 2 * HALO)
 
 
 def second_kernel(
-    starts, frames, swapped, crossed, dense, gains, own, weight, later_weight, first_in, first, second, state, wire, hidden, gain_pad
+    facts, halo, dense, gain_pad, own, weight, later_weight, first, second, state, wire, hidden
 ):
     cols = first.shape[1] - 2
-    channels = gains.shape[1]
-    keep = keep_factor(starts, frames)
-    fill_gain(gains, gain_pad)
+    channels = later_weight.shape[-1]
+    keep = facts[0][None, None, :]
     clear_borders(second)
-    own_in(own, second)
+    own_in(plain(own), second)
     hidden[:, 1] = jnp.zeros_like(hidden[:, 1])
 
     def enter(frame):
         def body(chunk):
-            main, rest = unpack_dense(received(swapped, crossed, dense_chunk(frame, chunk)))
+            main, rest = unpack_dense(halo[dense_chunk(frame, chunk)])
             main, rest = activate(main, rest, *load_gain(gain_pad, 0), channels)
             store_pieces(first, frame, chunk, main * keep, rest * keep)
 
         each_chunk(cols, body)
 
     each_frame(HALO, enter)
-    hidden_out(first, 0, weight.at[0], 0, hidden, gains, gain_pad, 1, second, None, NEW_FIRST, WHOLE)
+    hidden_out(first, 0, weight.at[0], 0, hidden, gain_pad, 1, second, None, NEW_FIRST, WHOLE)
 
     def finish(i, chunk, main, rest):
         main_in, rest_in = unpack_dense(dense[dense_chunk(HALO + i, chunk)])
@@ -329,15 +336,14 @@
 
 
 def third_kernel(
-    starts, frames, swapped, crossed, dense, gains, own, later_weight, second_in, second, third, state, wire, hidden, gain_pad
+    facts, halo, dense, gain_pad, own, later_weight, second, third, state, wire, hidden
 ):
-    channels = gains.shape[1]
-    keep = keep_factor(starts, frames)
-    fill_gain(gains, gain_pad)
+    channels = later_weight.shape[-1]
+    keep = facts[0][None, None, :]
     clear_borders(third)
-    own_in(own, third)
+    own_in(plain(own), third)
     hidden[:, 1] = jnp.zeros_like(hidden[:, 1])
-    halo_in(swapped, crossed, second, keep)
+    halo_in(plain(halo), second, keep)
 
     def finish(i, chunk, main, rest):
         main_in, rest_in = unpack_dense(dense[dense_chunk(i, chunk)])
@@ -347,45 +353,39 @@
         store_pieces(third, HALO + i, chunk, main, rest)
 
     residual_out(second, 0, later_weight.at[0], 1, hidden, NEW_FIRST, WHOLE, finish)
-    hidden_out(third, HALO, later_weight.at[1], 2, hidden, gains, gain_pad, 3, None, wire, NEW_FIRST, LAST_SPLIT)
-
-
-def live_factor(starts, frames, frame, span_frames):
-    span, own_start, own_frames = own_span(starts, frames)
-    return jnp.where((span - own_start) * span_frames + frame < own_frames, 1.0, 0.0).astype(jnp.float32)
+    hidden_out(third, HALO, later_weight.at[1], 2, hidden, gain_pad, 3, None, wire, NEW_FIRST, LAST_SPLIT)
 
 
 def fourth_kernel(
-    starts, frames, swapped, crossed, gains, own, later_weight, third_in, state, third, fourth, out, hidden, gain_pad
+    facts, swapped, crossed, gain_pad, own_odd, own_even, later_weight, third_in, state, third, fourth, out, hidden
 ):
-    keep = keep_factor(starts, frames)
-    fill_gain(gains, gain_pad)
+    keep = facts[0][None, None, :]
     clear_borders(fourth)
-    own_in(own, fourth)
+    own_in(by_place(own_even, own_odd), fourth)
     hidden[:, 1] = jnp.zeros_like(hidden[:, 1])
-    halo_in(swapped, crossed, third, keep)
-    hidden_out(third, 0, later_weight.at[1], 2, hidden, gains, gain_pad, 3, fourth, None, NEW_FIRST, WHOLE)
+    halo_in(by_place(crossed, swapped), third, keep)
+    hidden_out(third, 0, later_weight.at[1], 2, hidden, gain_pad, 3, fourth, None, NEW_FIRST, WHOLE)
 
     def finish(i, chunk, main, rest):
         main_in, rest_in = state_get(state, i, chunk)
-        live = live_factor(starts, frames, HALO + i, 2 * HALO)
+        live = facts[1 + HALO + i][None, None, :]
         pack_dense(out, i, chunk, (main + main_in) * live, (rest + rest_in) * live)
 
     residual_out(fourth, HALO, later_weight.at[2], 3, hidden, NEW_FIRST, LAST_SPLIT, finish)
 
 
 def fifth_kernel(
-    starts, frames, swapped, crossed, later_weight, fourth_in, state, later, fourth, out, hidden, stage, sems
+    facts, swapped, crossed, later_weight, fourth_in, state, later, fourth, out, hidden, stage, sems
 ):
-    keep = keep_factor(starts, frames)
+    keep = facts[0][None, None, :]
     copies = [pltpu.make_async_copy(later, out.at[pl.ds(HALO, HALO)], sems.at[0])]
     copies[0].start()
     hidden[:, 1] = jnp.zeros_like(hidden[:, 1])
-    halo_in(swapped, crossed, fourth, keep)
+    halo_in(by_place(crossed, swapped), fourth, keep)
 
     def finish(i, chunk, main, rest):
         main_in, rest_in = state_get(state, i, chunk)
-        live = live_factor(starts, frames, i, 2 * HALO)
+        live = facts[1 + i][None, None, :]
         pack_dense(stage, i, chunk, (main + main_in) * live, (rest + rest_in) * live)
 
     residual_out(fourth, 0, later_weight.at[2], 3, hidden, NEW_FIRST, LAST_SPLIT, finish)
@@ -407,8 +407,6 @@
     wire = jax.ShapeDtypeStruct((HALO, cols * 3 // 2, rows, LANES), bf16)
     state = jax.ShapeDtypeStruct((HALO, 2, cols, rows, LANES), bf16)
     hidden = VMEM((2 * HALO, 2, cols, rows, LANES), f32)
-    gain_pad = VMEM((layers, 2, LANES), f32)
-    smem = pl.BlockSpec(memory_space=pltpu.SMEM)
     vmem = pl.BlockSpec(memory_space=VMEM)
     hbm = pl.BlockSpec(memory_space=pltpu.HBM)
 
@@ -434,48 +432,119 @@
     dense = jax.ShapeDtypeStruct(features.shape, bf16)
     dense_half = jax.ShapeDtypeStruct((HALO, rows, merged), bf16)
     dma = pltpu.SemaphoreType.DMA
-    features_hbm, gains_hbm, weight_hbm = (
-        pltpu.with_memory_space_constraint(a, pltpu.HBM) for a in (features, gains, weight)
+    facts = jax.ShapeDtypeStruct((8, LANES), f32)
+    gain_rows = jax.ShapeDtypeStruct((layers, 2, LANES), f32)
+    in_hbm = [
+        pltpu.with_memory_space_constraint(a, pltpu.HBM)
+        for a in (features, gains, weight, video_start, video_frames)
+    ]
+    weight_hbm = in_hbm[2]
+    count = lax.axis_size("tm")
+    swap = [(i, i ^ 1) for i in range(count)]
+    cross = [(i, i + 1) for i in range(1, count - 1, 2)]
+
+    def half(body, odd, ins, specs, carried, outs, scratch, convs):
+        kernel = at_place(body, odd, len(ins), len(carried))
+        aliases = {len(ins) + n: index for n, index in enumerate(carried)}
+        arrays = (*ins, *carried.values())
+        return call(kernel, specs + [vmem] * len(carried), outs, scratch, convs, aliases)(*arrays)
+
+    def exchange(sent, even_step, swapped_of, next_step):
+        crossed = lax.ppermute(sent, "tm", cross)
+        even = even_step()
+        swapped = lax.ppermute(even[swapped_of], "tm", swap)
+        after = next_step(even, swapped)
+        return crossed, swapped, even, after
+
+    def stage(odd, carried):
+        outs = (pieces, dense_half, dense, weights(1), gain_rows, facts)
+        small = pltpu.SMEM(video_start.shape, jnp.int32)
+        scratch = [VMEM(gains.shape, f32), small, small, dma((6,))]
+        return half(stage_kernel, odd, in_hbm, [hbm] * 5, carried, outs, scratch, 0)
+
+    def step1(odd, staged, carried):
+        _, _, block, weight0, gain_rows, _ = staged
+        return half(
+            first_kernel,
+            odd,
+            (block, gain_rows, weight0, weight_hbm),
+            [vmem, vmem, vmem, hbm],
+            carried,
+            (pieces, wire, weights(layers - 1)),
+            [hidden, dma],
+            1,
+        )
+
+    def step2(odd, known, halo, block, own, weight0, later_weight, carried):
+        return half(
+            second_kernel,
+            odd,
+            (known[1], halo, block, known[0], own, weight0, later_weight),
+            [vmem] * 7,
+            carried,
+            (pieces, pieces, state, wire),
+            [hidden],
+            2,
+        )
+
+    def step3(odd, known, halo, block, own, later_weight, carried):
+        return half(
+            third_kernel,
+            odd,
+            (known[1], halo, block, known[0], own, later_weight),
+            [vmem] * 6,
+            carried,
+            (pieces, pieces, state, wire),
+            [hidden],
+            2,
+        )
+
+    odd0 = stage(True, {})
+    crossed0, swapped0, staged, odd1 = exchange(
+        odd0[1],
+        lambda: stage(False, {n: odd0[n] for n in (0, 2, 3, 4, 5)}),
+        1,
+        lambda staged, _: step1(True, staged, {0: staged[0]}),
     )
-    scalars = (video_start, video_frames)
-
-    first, wire0, features, weight0 = call(
-        stage_kernel,
-        [hbm, hbm, hbm],
-        (pieces, dense_half, dense, weights(1)),
-        [VMEM(gains.shape, f32), gain_pad, dma((4,))],
-        0,
-    )(features_hbm, gains_hbm, weight_hbm)
-    halo0 = passed_along(wire0, "tm", True)
-    first, wire1, later_weight = call(
-        first_kernel,
-        [vmem, vmem, vmem, hbm, vmem],
-        (pieces, wire, weights(layers - 1)),
-        [hidden, gain_pad, dma],
+    block, weight0, known = staged[2], staged[3], staged[4:]
+    crossed1, swapped1, even1, odd2 = exchange(
+        odd1[1],
+        lambda: step1(False, staged, {0: odd1[0], 2: odd1[2]}),
         1,
-        {4: 0},
-    )(features, gains, weight0, weight_hbm, first)
-    halo1 = passed_along(wire1, "tm", False)
-    _, second, state_late, wire2 = call(
-        second_kernel, [smem, smem] + [vmem] * 8, (pieces, pieces, state, wire), [hidden, gain_pad], 2, {9: 0}
-    )(*scalars, *halo0, features, gains, wire1, weight0, later_weight, first)
-    halo2 = passed_along(wire2, "tm", True)
-    _, third, state_early, wire3 = call(
-        third_kernel, [smem, smem] + [vmem] * 7, (pieces, pieces, state, wire), [hidden, gain_pad], 2, {8: 0}
-    )(*scalars, *halo1, features, gains, wire2, later_weight, second)
-    halo3 = passed_along(wire3, "tm", False)
-    _, fourth, later = call(
-        fourth_kernel, [smem, smem] + [vmem] * 7, (pieces, pieces, dense_half), [hidden, gain_pad], 2, {7: 0}
-    )(*scalars, *halo2, gains, wire3, later_weight, third, state_late)
+        lambda even, _: step2(True, known, swapped0, block, odd1[1], weight0, even[2], {0: even[0]}),
+    )
+    later_weight = even1[2]
+    crossed2, swapped2, even2, odd3 = exchange(
+        odd2[3],
+        lambda: step2(
+            False, known, crossed0, block, even1[1], weight0, later_weight, {0: odd2[0], 1: odd2[1], 2: odd2[2]}
+        ),
+        3,
+        lambda even, _: step3(True, known, swapped1, block, odd2[3], later_weight, {0: even[1]}),
+    )
+    state_late = even2[2]
+
+    def last_steps(even, swapped):
+        third = even[1]
+        return call(
+            fourth_kernel, [vmem] * 9, (pieces, pieces, dense_half), [hidden], 2, {7: 0}
+        )(known[1], swapped2, crossed2, known[0], odd3[3], even[3], later_weight, third, state_late)
+
+    crossed3, swapped3, even3, (_, fourth, later) = exchange(
+        odd3[3],
+        lambda: step3(False, known, crossed1, block, even2[3], later_weight, {0: odd3[0], 1: odd3[1], 2: odd3[2]}),
+        3,
+        last_steps,
+    )
     _, out = call(
         fifth_kernel,
-        [smem, smem] + [vmem] * 6,
+        [vmem] * 7,
         (pieces, dense),
         [hidden, VMEM(dense_half.shape, bf16), dma((1 + HALO,))],
         1,
-        {5: 0},
+        {4: 0},
         (vmem, hbm),
-    )(*scalars, *halo3, later_weight, fourth, state_early, later)
+    )(known[1], swapped3, crossed3, later_weight, fourth, even3[2], later)
     return out
 
 

time: 42.2 us -> 40.4 us (0.957)
  Pallas kernels: 26 us -> 24.4 us
    pallas_call x6 -> x10, Pallas kernels: 26 us -> 24.4 us  [the longest x8 16.3 us: half(): call(kernel, specs + [vmem] * len(carried), outs, scratch, convs, aliases)]
  transfers between devices with their start and end apart: 8 -> 8, of which waited for: 0 -> 0; matrix products, arithmetic and copies ran while one was open for 0% -> 0% of each run, Pallas kernels for 48% -> 47%
where the time goes in v3:
time: 40.4 us; the launch traced here: 40.2 us
  Pallas kernels  24.4 us (60%)
  starting transfers between devices  15.4 us (38%)
    pallas_call x8, Pallas kernels, half(): call(kernel, specs + [vmem] * len(carried), outs, scratch, convs, aliases)  16.3 us
    ppermute x4, starting transfers between devices, exchange(): crossed = lax.ppermute(sent, 'tm', cross)  15.1 us
    pallas_call x1, Pallas kernels, last_steps(): call(fourth_kernel, [vmem] * 9, (pieces, pieces, dense_half), [hidden], 2...  4.93 us
    pallas_call x1, Pallas kernels, local(): call(fifth_kernel, [vmem] * 7, (pieces, dense), [hidden, VMEM(dense_half....  3.15 us
  transfers between devices with their start and end apart: 8, of which 0 were waited for; matrix products, arithmetic and copies ran while one was open for 0% of the time, Pallas kernels for 47%

profile of v3, /device:TPU:1, one launch (start us, length us, event | category | flops | bytes accessed | tf_op | source)
XLA Modules:
  0.0 40.2 jit_solution(15121686909246922993)
XLA Ops:
  0.0 2.1 %shard_map.55 = (bf16[6,26,16,640]{3,2,1,0:T(8,128)(2,1)S(1)}, bf16[2,16,4608]{2,1,0:T(8,128)(2,1)S(1)}, bf16[4,16,4608]{2,1,0:T(8,128)(2,1)S(1)}, bf16[1,27,192...) custom-call(bf16[4,16,4608]{2,1,0:T(8,128)(2,1)} %refs_0_.3, f32[4,192]{1,0:T(4,128)} %refs_1_.3, ...), custom_call_target="tpu_custom_call" | custom-call | bytes 4194304 | tf_op jit(solution)/shard_map/pallas_call | solution.py:450
  2.1 0.1 shard_map.56
  2.2 0.1 collective-permute-start.2
  2.3 4.5 %collective-permute-start.1 = (bf16[2,16,4608]{2,1,0:T(8,128)(2,1)S(1)}, bf16[2,16,4608]{2,1,0:T(8,128)(2,1)S(1)}, u32[]{:S(2)}, u32[]{:S(2)}) collective-permute-start(bf16[2,16,4608]{2,1,0:T(8,128)(2,1)S(1)} %get-tuple-element.51), channel_id=1, source_target_pairs={{1,2},{3,4},{5,6},{7,8},{9,10},{11,12},{13,14},{17,18},{19,20},{21... | collective-permute-start | bytes 884744 | tf_op jit(solution)/shard_map/ppermute | solution.py:453
  6.8 3.3 %shard_map.57 = (bf16[6,26,16,640]{3,2,1,0:T(8,128)(2,1)S(1)}, bf16[2,36,16,128]{3,2,1,0:T(8,128)(2,1)S(1)}, bf16[3,27,192,192]{3,2,1,0:T(8,128)(2,1)S(1)}) custom-call(bf16[4,16,4608]{2,1,0:T(8,128)(2,1)S(1)} %get-tuple-element.46.refs_0_.refs_2_, f32[4,2,128]{2,1,0:T(2,128)S(1)} %get-tuple-element.47.refs_1_.refs_3_.gain_pad, ...), custom_call_target="tpu_custom_call", output_to_operand_aliasing={{0}: (4, {})} | custom-call | flops 1528823808 | bytes 4194304 | tf_op jit(solution)/shard_map/pallas_call | solution.py:450
  10.1 0.1 collective-permute-start.3
  10.2 3.5 %collective-permute-start = (bf16[2,36,16,128]{3,2,1,0:T(8,128)(2,1)S(1)}, bf16[2,36,16,128]{3,2,1,0:T(8,128)(2,1)S(1)}, u32[]{:S(2)}, u32[]{:S(2)}) collective-permute-start(bf16[2,36,16,128]{3,2,1,0:T(8,128)(2,1)S(1)} %get-tuple-element.50.refs_4_), channel_id=1, source_target_pairs={{1,2},{3,4},{5,6},{7,8},{9,10},{11,12},{13,14},{17,18},{19,20},{21... | collective-permute-start | bytes 884744 | tf_op jit(solution)/shard_map/ppermute | solution.py:453
  13.8 0.0 collective-permute-done.2.refs_1_
  13.8 5.2 %shard_map.59 = (bf16[6,26,16,640]{3,2,1,0:T(8,128)(2,1)S(1)}, bf16[6,26,16,640]{3,2,1,0:T(8,128)(2,1)S(1)}, bf16[2,2,24,16,128]{4,3,2,1,0:T(8,128)(2,1)S(1)}, bf16[2,36,16,128]{3,2,1,0:T(8,128)(2,1)S(1)}) custom-call(f32[8,128]{1,0:T(8,128)S(1)} %get-tuple-element.45.refs_0_.facts, ...), custom_call_target="tpu_custom_call", output_to_operand_aliasing={{0}: (7, {})} | custom-call | flops 3057647616 | bytes 4194304 | tf_op jit(solution)/shard_map/pallas_call | solution.py:450
  19.0 0.0 collective-permute-done.1.refs_1_
  19.0 0.2 shard_map.60
  19.2 0.1 collective-permute-start.6
  19.3 3.5 %collective-permute-start.7 = (bf16[2,36,16,128]{3,2,1,0:T(8,128)(2,1)S(1)}, bf16[2,36,16,128]{3,2,1,0:T(8,128)(2,1)S(1)}, u32[]{:S(2)}, u32[]{:S(2)}) collective-permute-start(bf16[2,36,16,128]{3,2,1,0:T(8,128)(2,1)S(1)} %get-tuple-element.62.refs_4_), channel_id=1, source_target_pairs={{1,2},{3,4},{5,6},{7,8},{9,10},{11,12},{13,14},{17,18},{19,20},{21... | collective-permute-start | bytes 884744 | tf_op jit(solution)/shard_map/ppermute | solution.py:453
  22.8 0.0 collective-permute-done.3.refs_1_
  22.8 5.1 %shard_map.61 = (bf16[6,26,16,640]{3,2,1,0:T(8,128)(2,1)S(1)}, bf16[6,26,16,640]{3,2,1,0:T(8,128)(2,1)S(1)}, bf16[2,2,24,16,128]{4,3,2,1,0:T(8,128)(2,1)S(1)}, bf16[2,36,16,128]{3,2,1,0:T(8,128)(2,1)S(1)}) custom-call(f32[8,128]{1,0:T(8,128)S(1)} %get-tuple-element.45.refs_0_.facts, ...), custom_call_target="tpu_custom_call", output_to_operand_aliasing={{0}: (6, {})} | custom-call | flops 3057647616 | bytes 4194304 | tf_op jit(solution)/shard_map/pallas_call | solution.py:450
  28.0 0.0 collective-permute-done.refs_1_
  28.0 0.2 shard_map.62
  28.2 0.1 collective-permute-start.4
  28.3 3.5 %collective-permute-start.5 = (bf16[2,36,16,128]{3,2,1,0:T(8,128)(2,1)S(1)}, bf16[2,36,16,128]{3,2,1,0:T(8,128)(2,1)S(1)}, u32[]{:S(2)}, u32[]{:S(2)}) collective-permute-start(bf16[2,36,16,128]{3,2,1,0:T(8,128)(2,1)S(1)} %get-tuple-element.68.own_odd), channel_id=1, source_target_pairs={{1,2},{3,4},{5,6},{7,8},{9,10},{11,12},{13,14},{17,18},{19,20},{21... | collective-permute-start | bytes 884744 | tf_op jit(solution)/shard_map/ppermute | solution.py:453
  31.9 0.0 collective-permute-done.6.swapped
  31.9 0.0 collective-permute-done.7.crossed
  31.9 4.9 %shard_map.63 = (bf16[6,26,16,640]{3,2,1,0:T(8,128)(2,1)S(1)}, bf16[6,26,16,640]{3,2,1,0:T(8,128)(2,1)S(1)}, bf16[2,16,4608]{2,1,0:T(8,128)(2,1)S(1)}) custom-call(f32[8,128]{1,0:T(8,128)S(1)} %get-tuple-element.45.refs_0_.facts, bf16[2,36,16,128]{3,2,1,0:T(8,128)(2,1)S(1)} %collective-permute-done.6.swapped, ...), custom_call_target="tpu_custom_call", output_to_operand_aliasing={{0}: (7, {})} | custom-call | flops 3057647616 | bytes 4194304 | tf_op jit(solution)/shard_map/pallas_call | solution.py:529
  36.8 0.0 collective-permute-done.4.swapped
  36.8 0.0 collective-permute-done.5.crossed
  36.8 3.1 %shard_map.64 = (bf16[6,26,16,640]{3,2,1,0:T(8,128)(2,1)S(1)}, bf16[4,16,4608]{2,1,0:T(8,128)(2,1)}) custom-call(f32[8,128]{1,0:T(8,128)S(1)} %get-tuple-element.45.refs_0_.facts, bf16[2,36,16,128]{3,2,1,0:T(8,128)(2,1)S(1)} %collective-permute-done.4.swapped, ...), custom_call_target="tpu_custom_call", output_to_operand_aliasing={{0}: (4, {})} | custom-call | flops 1528823808 | bytes 4194304 | tf_op jit(solution)/shard_map/pallas_call | solution.py:539
  (1 shorter events, 0.0 us)
Async XLA Ops:
  2.2 11.6 %collective-permute-start.2 = (bf16[2,16,4608]{2,1,0:T(8,128)(2,1)S(1)}, bf16[2,16,4608]{2,1,0:T(8,128)(2,1)S(1)}, u32[]{:S(2)}, u32[]{:S(2)}) collective-permute-start(bf16[2,16,4608]{2,1,0:T(8,128)(2,1)S(1)} %get-tuple-element.56), channel_id=1, source_target_pairs={{0,1},{1,0},{2,3},{3,2},{4,5},{5,4},{6,7},{7,6},{8,9},{9,8},{10,11... | collective-permute-start | bytes 884744 | tf_op jit(solution)/shard_map/ppermute | solution.py:455
  2.3 16.7 %collective-permute-start.1 = (bf16[2,16,4608]{2,1,0:T(8,128)(2,1)S(1)}, bf16[2,16,4608]{2,1,0:T(8,128)(2,1)S(1)}, u32[]{:S(2)}, u32[]{:S(2)}) collective-permute-start(bf16[2,16,4608]{2,1,0:T(8,128)(2,1)S(1)} %get-tuple-element.51), channel_id=1, source_target_pairs={{1,2},{3,4},{5,6},{7,8},{9,10},{11,12},{13,14},{17,18},{19,20},{21... | collective-permute-start | bytes 884744 | tf_op jit(solution)/shard_map/ppermute | solution.py:453
  10.1 12.7 %collective-permute-start.3 = (bf16[2,36,16,128]{3,2,1,0:T(8,128)(2,1)S(1)}, bf16[2,36,16,128]{3,2,1,0:T(8,128)(2,1)S(1)}, u32[]{:S(2)}, u32[]{:S(2)}) collective-permute-start(bf16[2,36,16,128]{3,2,1,0:T(8,128)(2,1)S(1)} %get-tuple-element.54.refs_4_), channel_id=1, source_target_pairs={{0,1},{1,0},{2,3},{3,2},{4,5},{5,4},{6,7},{7,6},{8,9},{9,8},{10,11... | collective-permute-start | bytes 884744 | tf_op jit(solution)/shard_map/ppermute | solution.py:455
  10.2 17.8 %collective-permute-start = (bf16[2,36,16,128]{3,2,1,0:T(8,128)(2,1)S(1)}, bf16[2,36,16,128]{3,2,1,0:T(8,128)(2,1)S(1)}, u32[]{:S(2)}, u32[]{:S(2)}) collective-permute-start(bf16[2,36,16,128]{3,2,1,0:T(8,128)(2,1)S(1)} %get-tuple-element.50.refs_4_), channel_id=1, source_target_pairs={{1,2},{3,4},{5,6},{7,8},{9,10},{11,12},{13,14},{17,18},{19,20},{21... | collective-permute-start | bytes 884744 | tf_op jit(solution)/shard_map/ppermute | solution.py:453
  19.2 12.6 %collective-permute-start.6 = (bf16[2,36,16,128]{3,2,1,0:T(8,128)(2,1)S(1)}, bf16[2,36,16,128]{3,2,1,0:T(8,128)(2,1)S(1)}, u32[]{:S(2)}, u32[]{:S(2)}) collective-permute-start(bf16[2,36,16,128]{3,2,1,0:T(8,128)(2,1)S(1)} %get-tuple-element.61.refs_4_), channel_id=1, source_target_pairs={{0,1},{1,0},{2,3},{3,2},{4,5},{5,4},{6,7},{7,6},{8,9},{9,8},{10,11... | collective-permute-start | bytes 884744 | tf_op jit(solution)/shard_map/ppermute | solution.py:455
  19.3 12.6 %collective-permute-start.7 = (bf16[2,36,16,128]{3,2,1,0:T(8,128)(2,1)S(1)}, bf16[2,36,16,128]{3,2,1,0:T(8,128)(2,1)S(1)}, u32[]{:S(2)}, u32[]{:S(2)}) collective-permute-start(bf16[2,36,16,128]{3,2,1,0:T(8,128)(2,1)S(1)} %get-tuple-element.62.refs_4_), channel_id=1, source_target_pairs={{1,2},{3,4},{5,6},{7,8},{9,10},{11,12},{13,14},{17,18},{19,20},{21... | collective-permute-start | bytes 884744 | tf_op jit(solution)/shard_map/ppermute | solution.py:453
  28.2 8.6 %collective-permute-start.4 = (bf16[2,36,16,128]{3,2,1,0:T(8,128)(2,1)S(1)}, bf16[2,36,16,128]{3,2,1,0:T(8,128)(2,1)S(1)}, u32[]{:S(2)}, u32[]{:S(2)}) collective-permute-start(bf16[2,36,16,128]{3,2,1,0:T(8,128)(2,1)S(1)} %get-tuple-element.67.own_even), channel_id=1, source_target_pairs={{0,1},{1,0},{2,3},{3,2},{4,5},{5,4},{6,7},{7,6},{8,9},{9,8},{10,11... | collective-permute-start | bytes 884744 | tf_op jit(solution)/shard_map/ppermute | solution.py:455
  28.3 8.5 %collective-permute-start.5 = (bf16[2,36,16,128]{3,2,1,0:T(8,128)(2,1)S(1)}, bf16[2,36,16,128]{3,2,1,0:T(8,128)(2,1)S(1)}, u32[]{:S(2)}, u32[]{:S(2)}) collective-permute-start(bf16[2,36,16,128]{3,2,1,0:T(8,128)(2,1)S(1)} %get-tuple-element.68.own_odd), channel_id=1, source_target_pairs={{1,2},{3,4},{5,6},{7,8},{9,10},{11,12},{13,14},{17,18},{19,20},{21... | collective-permute-start | bytes 884744 | tf_op jit(solution)/shard_map/ppermute | solution.py:453

commit v4 on v3

--- a/solution.py
+++ b/solution.py
@@ -9,11 +9,12 @@
 LANES = 128
 HALO = 2
 STEP = 4
-STAGED = 1
+STAGED = 0
 OLD_FIRST = (0, 1, 2)
 NEW_FIRST = (2, 1, 0)
-WHOLE = (1, 1)
-LAST_SPLIT = (1, 1)
+WHOLE = 1
+LAST_SPLIT = 2
+END_SPLIT = 2
 VMEM = pltpu.VMEM
 
 
@@ -242,15 +243,15 @@
     hidden[:, 1] = jnp.zeros_like(hidden[:, 1])
     for frame in range(STAGED, dense.shape[0]):
         dense_in(dense, first, frame, gain_pad, weight.shape[-1])
-    hidden_out(first, HALO, weight.at[0], 0, hidden, gain_pad, 1, None, wire, OLD_FIRST, LAST_SPLIT)
+    hidden_out(first, HALO, weight.at[0], 0, hidden, gain_pad, 1, None, wire, OLD_FIRST, WHOLE)
     copy.wait()
 
 
 def convolve_frames(source, base, weight, layer, hidden, taps, splits, finish):
     cols = source.shape[1] - 2
-    for i in range(HALO):
-        part = cols // splits[i]
-        for first_col in range(0, cols, part):
+    part = cols // splits
+    for first_col in range(0, cols, part):
+        for i in range(HALO):
             slot = 2 * (layer % 2) + i
             convolve(source, base + i, weight, hidden, slot, first_col, part, taps)
             for chunk in range(first_col // STEP, (first_col + part) // STEP):
@@ -382,16 +383,21 @@
     copies[0].start()
     hidden[:, 1] = jnp.zeros_like(hidden[:, 1])
     halo_in(by_place(crossed, swapped), fourth, keep)
+    width = stage.shape[2] // END_SPLIT
+    chunks = (fourth.shape[1] - 2) // (STEP * END_SPLIT)
 
     def finish(i, chunk, main, rest):
         main_in, rest_in = state_get(state, i, chunk)
         live = facts[1 + i][None, None, :]
         pack_dense(stage, i, chunk, (main + main_in) * live, (rest + rest_in) * live)
-
-    residual_out(fourth, 0, later_weight.at[2], 3, hidden, NEW_FIRST, LAST_SPLIT, finish)
-    for i in range(HALO):
-        copies.append(pltpu.make_async_copy(stage.at[i], out.at[i], sems.at[1 + i]))
-        copies[-1].start()
+        if (chunk + 1) % chunks == 0:
+            part = chunk // chunks
+            lanes = pl.ds(part * width, width)
+            sem = sems.at[1 + HALO * part + i]
+            copies.append(pltpu.make_async_copy(stage.at[i, :, lanes], out.at[i, :, lanes], sem))
+            copies[-1].start()
+
+    residual_out(fourth, 0, later_weight.at[2], 3, hidden, NEW_FIRST, END_SPLIT, finish)
     for copy in copies:
         copy.wait()
 
@@ -540,7 +546,7 @@
         fifth_kernel,
         [vmem] * 7,
         (pieces, dense),
-        [hidden, VMEM(dense_half.shape, bf16), dma((1 + HALO,))],
+        [hidden, VMEM(dense_half.shape, bf16), dma((1 + HALO * END_SPLIT,))],
         1,
         {4: 0},
         (vmem, hbm),

time: 40.4 us -> 39.9 us (0.988)
  Pallas kernels: 24.4 us -> 23.9 us
where the time goes in v4:
time: 39.9 us; the launch traced here: 39.7 us
  Pallas kernels  23.9 us (60%)
  starting transfers between devices  15.4 us (39%)
    pallas_call x8, Pallas kernels, half(): call(kernel, specs + [vmem] * len(carried), outs, scratch, convs, aliases)  16 us
    ppermute x4, starting transfers between devices, exchange(): crossed = lax.ppermute(sent, 'tm', cross)  15.1 us
    pallas_call x1, Pallas kernels, last_steps(): call(fourth_kernel, [vmem] * 9, (pieces, pieces, dense_half), [hidden], 2...  4.75 us
    pallas_call x1, Pallas kernels, local(): call(fifth_kernel, [vmem] * 7, (pieces, dense), [hidden, VMEM(dense_half....  3.14 us
  transfers between devices with their start and end apart: 8, of which 0 were waited for; matrix products, arithmetic and copies ran while one was open for 0% of the time, Pallas kernels for 47%

profile of v4, /device:TPU:1, one launch (start us, length us, event | category | flops | bytes accessed | tf_op | source)
XLA Modules:
  0.0 39.7 jit_solution(5901312837208435945)
XLA Ops:
  0.0 2.1 %shard_map.55 = (bf16[6,26,16,640]{3,2,1,0:T(8,128)(2,1)S(1)}, bf16[2,16,4608]{2,1,0:T(8,128)(2,1)S(1)}, bf16[4,16,4608]{2,1,0:T(8,128)(2,1)S(1)}, bf16[1,27,192...) custom-call(bf16[4,16,4608]{2,1,0:T(8,128)(2,1)} %refs_0_.3, f32[4,192]{1,0:T(4,128)} %refs_1_.3, ...), custom_call_target="tpu_custom_call" | custom-call | bytes 4194304 | tf_op jit(solution)/shard_map/pallas_call | solution.py:456
  2.1 0.1 shard_map.56
  2.2 0.1 collective-permute-start.2
  2.3 4.5 %collective-permute-start.1 = (bf16[2,16,4608]{2,1,0:T(8,128)(2,1)S(1)}, bf16[2,16,4608]{2,1,0:T(8,128)(2,1)S(1)}, u32[]{:S(2)}, u32[]{:S(2)}) collective-permute-start(bf16[2,16,4608]{2,1,0:T(8,128)(2,1)S(1)} %get-tuple-element.51), channel_id=1, source_target_pairs={{1,2},{3,4},{5,6},{7,8},{9,10},{11,12},{13,14},{17,18},{19,20},{21... | collective-permute-start | bytes 884744 | tf_op jit(solution)/shard_map/ppermute | solution.py:459
  6.8 3.3 %shard_map.57 = (bf16[6,26,16,640]{3,2,1,0:T(8,128)(2,1)S(1)}, bf16[2,36,16,128]{3,2,1,0:T(8,128)(2,1)S(1)}, bf16[3,27,192,192]{3,2,1,0:T(8,128)(2,1)S(1)}) custom-call(bf16[4,16,4608]{2,1,0:T(8,128)(2,1)S(1)} %get-tuple-element.46.refs_0_.refs_2_, f32[4,2,128]{2,1,0:T(2,128)S(1)} %get-tuple-element.47.refs_1_.refs_3_.gain_pad, ...), custom_call_target="tpu_custom_call", output_to_operand_aliasing={{0}: (4, {})} | custom-call | flops 1528823808 | bytes 4194304 | tf_op jit(solution)/shard_map/pallas_call | solution.py:456
  10.1 0.1 collective-permute-start.3
  10.2 3.5 %collective-permute-start = (bf16[2,36,16,128]{3,2,1,0:T(8,128)(2,1)S(1)}, bf16[2,36,16,128]{3,2,1,0:T(8,128)(2,1)S(1)}, u32[]{:S(2)}, u32[]{:S(2)}) collective-permute-start(bf16[2,36,16,128]{3,2,1,0:T(8,128)(2,1)S(1)} %get-tuple-element.50.refs_4_), channel_id=1, source_target_pairs={{1,2},{3,4},{5,6},{7,8},{9,10},{11,12},{13,14},{17,18},{19,20},{21... | collective-permute-start | bytes 884744 | tf_op jit(solution)/shard_map/ppermute | solution.py:459
  13.8 0.0 collective-permute-done.2.refs_1_
  13.8 5.0 %shard_map.59 = (bf16[6,26,16,640]{3,2,1,0:T(8,128)(2,1)S(1)}, bf16[6,26,16,640]{3,2,1,0:T(8,128)(2,1)S(1)}, bf16[2,2,24,16,128]{4,3,2,1,0:T(8,128)(2,1)S(1)}, bf16[2,36,16,128]{3,2,1,0:T(8,128)(2,1)S(1)}) custom-call(f32[8,128]{1,0:T(8,128)S(1)} %get-tuple-element.45.refs_0_.facts, ...), custom_call_target="tpu_custom_call", output_to_operand_aliasing={{0}: (7, {})} | custom-call | flops 3057647616 | bytes 4194304 | tf_op jit(solution)/shard_map/pallas_call | solution.py:456
  18.8 0.0 collective-permute-done.1.refs_1_
  18.8 0.2 shard_map.60
  19.0 0.1 collective-permute-start.6
  19.1 3.5 %collective-permute-start.7 = (bf16[2,36,16,128]{3,2,1,0:T(8,128)(2,1)S(1)}, bf16[2,36,16,128]{3,2,1,0:T(8,128)(2,1)S(1)}, u32[]{:S(2)}, u32[]{:S(2)}) collective-permute-start(bf16[2,36,16,128]{3,2,1,0:T(8,128)(2,1)S(1)} %get-tuple-element.62.refs_4_), channel_id=1, source_target_pairs={{1,2},{3,4},{5,6},{7,8},{9,10},{11,12},{13,14},{17,18},{19,20},{21... | collective-permute-start | bytes 884744 | tf_op jit(solution)/shard_map/ppermute | solution.py:459
  22.6 0.0 collective-permute-done.3.refs_1_
  22.7 5.1 %shard_map.61 = (bf16[6,26,16,640]{3,2,1,0:T(8,128)(2,1)S(1)}, bf16[6,26,16,640]{3,2,1,0:T(8,128)(2,1)S(1)}, bf16[2,2,24,16,128]{4,3,2,1,0:T(8,128)(2,1)S(1)}, bf16[2,36,16,128]{3,2,1,0:T(8,128)(2,1)S(1)}) custom-call(f32[8,128]{1,0:T(8,128)S(1)} %get-tuple-element.45.refs_0_.facts, ...), custom_call_target="tpu_custom_call", output_to_operand_aliasing={{0}: (6, {})} | custom-call | flops 3057647616 | bytes 4194304 | tf_op jit(solution)/shard_map/pallas_call | solution.py:456
  27.7 0.0 collective-permute-done.refs_1_
  27.7 0.2 shard_map.62
  28.0 0.1 collective-permute-start.4
  28.1 3.5 %collective-permute-start.5 = (bf16[2,36,16,128]{3,2,1,0:T(8,128)(2,1)S(1)}, bf16[2,36,16,128]{3,2,1,0:T(8,128)(2,1)S(1)}, u32[]{:S(2)}, u32[]{:S(2)}) collective-permute-start(bf16[2,36,16,128]{3,2,1,0:T(8,128)(2,1)S(1)} %get-tuple-element.68.own_odd), channel_id=1, source_target_pairs={{1,2},{3,4},{5,6},{7,8},{9,10},{11,12},{13,14},{17,18},{19,20},{21... | collective-permute-start | bytes 884744 | tf_op jit(solution)/shard_map/ppermute | solution.py:459
  31.6 0.0 collective-permute-done.6.swapped
  31.6 0.0 collective-permute-done.7.crossed
  31.6 4.8 %shard_map.63 = (bf16[6,26,16,640]{3,2,1,0:T(8,128)(2,1)S(1)}, bf16[6,26,16,640]{3,2,1,0:T(8,128)(2,1)S(1)}, bf16[2,16,4608]{2,1,0:T(8,128)(2,1)S(1)}) custom-call(f32[8,128]{1,0:T(8,128)S(1)} %get-tuple-element.45.refs_0_.facts, bf16[2,36,16,128]{3,2,1,0:T(8,128)(2,1)S(1)} %collective-permute-done.6.swapped, ...), custom_call_target="tpu_custom_call", output_to_operand_aliasing={{0}: (7, {})} | custom-call | flops 3057647616 | bytes 4194304 | tf_op jit(solution)/shard_map/pallas_call | solution.py:535
  36.4 0.0 collective-permute-done.4.swapped
  36.4 0.0 collective-permute-done.5.crossed
  36.4 3.1 %shard_map.64 = (bf16[6,26,16,640]{3,2,1,0:T(8,128)(2,1)S(1)}, bf16[4,16,4608]{2,1,0:T(8,128)(2,1)}) custom-call(f32[8,128]{1,0:T(8,128)S(1)} %get-tuple-element.45.refs_0_.facts, bf16[2,36,16,128]{3,2,1,0:T(8,128)(2,1)S(1)} %collective-permute-done.4.swapped, ...), custom_call_target="tpu_custom_call", output_to_operand_aliasing={{0}: (4, {})} | custom-call | flops 1528823808 | bytes 4194304 | tf_op jit(solution)/shard_map/pallas_call | solution.py:545
  (1 shorter events, 0.0 us)
Async XLA Ops:
  2.2 11.6 %collective-permute-start.2 = (bf16[2,16,4608]{2,1,0:T(8,128)(2,1)S(1)}, bf16[2,16,4608]{2,1,0:T(8,128)(2,1)S(1)}, u32[]{:S(2)}, u32[]{:S(2)}) collective-permute-start(bf16[2,16,4608]{2,1,0:T(8,128)(2,1)S(1)} %get-tuple-element.56), channel_id=1, source_target_pairs={{0,1},{1,0},{2,3},{3,2},{4,5},{5,4},{6,7},{7,6},{8,9},{9,8},{10,11... | collective-permute-start | bytes 884744 | tf_op jit(solution)/shard_map/ppermute | solution.py:461
  2.3 16.5 %collective-permute-start.1 = (bf16[2,16,4608]{2,1,0:T(8,128)(2,1)S(1)}, bf16[2,16,4608]{2,1,0:T(8,128)(2,1)S(1)}, u32[]{:S(2)}, u32[]{:S(2)}) collective-permute-start(bf16[2,16,4608]{2,1,0:T(8,128)(2,1)S(1)} %get-tuple-element.51), channel_id=1, source_target_pairs={{1,2},{3,4},{5,6},{7,8},{9,10},{11,12},{13,14},{17,18},{19,20},{21... | collective-permute-start | bytes 884744 | tf_op jit(solution)/shard_map/ppermute | solution.py:459
  10.1 12.5 %collective-permute-start.3 = (bf16[2,36,16,128]{3,2,1,0:T(8,128)(2,1)S(1)}, bf16[2,36,16,128]{3,2,1,0:T(8,128)(2,1)S(1)}, u32[]{:S(2)}, u32[]{:S(2)}) collective-permute-start(bf16[2,36,16,128]{3,2,1,0:T(8,128)(2,1)S(1)} %get-tuple-element.54.refs_4_), channel_id=1, source_target_pairs={{0,1},{1,0},{2,3},{3,2},{4,5},{5,4},{6,7},{7,6},{8,9},{9,8},{10,11... | collective-permute-start | bytes 884744 | tf_op jit(solution)/shard_map/ppermute | solution.py:461
  10.2 17.5 %collective-permute-start = (bf16[2,36,16,128]{3,2,1,0:T(8,128)(2,1)S(1)}, bf16[2,36,16,128]{3,2,1,0:T(8,128)(2,1)S(1)}, u32[]{:S(2)}, u32[]{:S(2)}) collective-permute-start(bf16[2,36,16,128]{3,2,1,0:T(8,128)(2,1)S(1)} %get-tuple-element.50.refs_4_), channel_id=1, source_target_pairs={{1,2},{3,4},{5,6},{7,8},{9,10},{11,12},{13,14},{17,18},{19,20},{21... | collective-permute-start | bytes 884744 | tf_op jit(solution)/shard_map/ppermute | solution.py:459
  19.0 12.6 %collective-permute-start.6 = (bf16[2,36,16,128]{3,2,1,0:T(8,128)(2,1)S(1)}, bf16[2,36,16,128]{3,2,1,0:T(8,128)(2,1)S(1)}, u32[]{:S(2)}, u32[]{:S(2)}) collective-permute-start(bf16[2,36,16,128]{3,2,1,0:T(8,128)(2,1)S(1)} %get-tuple-element.61.refs_4_), channel_id=1, source_target_pairs={{0,1},{1,0},{2,3},{3,2},{4,5},{5,4},{6,7},{7,6},{8,9},{9,8},{10,11... | collective-permute-start | bytes 884744 | tf_op jit(solution)/shard_map/ppermute | solution.py:461
  19.1 12.5 %collective-permute-start.7 = (bf16[2,36,16,128]{3,2,1,0:T(8,128)(2,1)S(1)}, bf16[2,36,16,128]{3,2,1,0:T(8,128)(2,1)S(1)}, u32[]{:S(2)}, u32[]{:S(2)}) collective-permute-start(bf16[2,36,16,128]{3,2,1,0:T(8,128)(2,1)S(1)} %get-tuple-element.62.refs_4_), channel_id=1, source_target_pairs={{1,2},{3,4},{5,6},{7,8},{9,10},{11,12},{13,14},{17,18},{19,20},{21... | collective-permute-start | bytes 884744 | tf_op jit(solution)/shard_map/ppermute | solution.py:459
  28.0 8.4 %collective-permute-start.4 = (bf16[2,36,16,128]{3,2,1,0:T(8,128)(2,1)S(1)}, bf16[2,36,16,128]{3,2,1,0:T(8,128)(2,1)S(1)}, u32[]{:S(2)}, u32[]{:S(2)}) collective-permute-start(bf16[2,36,16,128]{3,2,1,0:T(8,128)(2,1)S(1)} %get-tuple-element.67.own_even), channel_id=1, source_target_pairs={{0,1},{1,0},{2,3},{3,2},{4,5},{5,4},{6,7},{7,6},{8,9},{9,8},{10,11... | collective-permute-start | bytes 884744 | tf_op jit(solution)/shard_map/ppermute | solution.py:461
  28.1 8.3 %collective-permute-start.5 = (bf16[2,36,16,128]{3,2,1,0:T(8,128)(2,1)S(1)}, bf16[2,36,16,128]{3,2,1,0:T(8,128)(2,1)S(1)}, u32[]{:S(2)}, u32[]{:S(2)}) collective-permute-start(bf16[2,36,16,128]{3,2,1,0:T(8,128)(2,1)S(1)} %get-tuple-element.68.own_odd), channel_id=1, source_target_pairs={{1,2},{3,4},{5,6},{7,8},{9,10},{11,12},{13,14},{17,18},{19,20},{21... | collective-permute-start | bytes 884744 | tf_op jit(solution)/shard_map/ppermute | solution.py:459

commit v5 on v4

--- a/solution.py
+++ b/solution.py
@@ -306,11 +306,13 @@
 
 
 def second_kernel(
-    facts, halo, dense, gain_pad, own, weight, later_weight, first, second, state, wire, hidden
+    facts, halo, dense, gain_pad, own, weight, later_weight, weight_hbm, first, second, state, wire, last_weight, hidden, sem
 ):
     cols = first.shape[1] - 2
     channels = later_weight.shape[-1]
     keep = facts[0][None, None, :]
+    copy = pltpu.make_async_copy(weight_hbm.at[pl.ds(2, last_weight.shape[0])], last_weight, sem)
+    copy.start()
     clear_borders(second)
     own_in(plain(own), second)
     hidden[:, 1] = jnp.zeros_like(hidden[:, 1])
@@ -334,10 +336,11 @@
         pack_wire(wire, i, chunk, main, rest)
 
     residual_out(second, HALO, later_weight.at[0], 1, hidden, NEW_FIRST, LAST_SPLIT, finish)
+    copy.wait()
 
 
 def third_kernel(
-    facts, halo, dense, gain_pad, own, later_weight, second, third, state, wire, hidden
+    facts, halo, dense, gain_pad, own, later_weight, last_weight, second, third, state, wire, hidden
 ):
     channels = later_weight.shape[-1]
     keep = facts[0][None, None, :]
@@ -354,29 +357,29 @@
         store_pieces(third, HALO + i, chunk, main, rest)
 
     residual_out(second, 0, later_weight.at[0], 1, hidden, NEW_FIRST, WHOLE, finish)
-    hidden_out(third, HALO, later_weight.at[1], 2, hidden, gain_pad, 3, None, wire, NEW_FIRST, LAST_SPLIT)
+    hidden_out(third, HALO, last_weight.at[0], 2, hidden, gain_pad, 3, None, wire, NEW_FIRST, LAST_SPLIT)
 
 
 def fourth_kernel(
-    facts, swapped, crossed, gain_pad, own_odd, own_even, later_weight, third_in, state, third, fourth, out, hidden
+    facts, swapped, crossed, gain_pad, own_odd, own_even, last_weight, third_in, state, third, fourth, out, hidden
 ):
     keep = facts[0][None, None, :]
     clear_borders(fourth)
     own_in(by_place(own_even, own_odd), fourth)
     hidden[:, 1] = jnp.zeros_like(hidden[:, 1])
     halo_in(by_place(crossed, swapped), third, keep)
-    hidden_out(third, 0, later_weight.at[1], 2, hidden, gain_pad, 3, fourth, None, NEW_FIRST, WHOLE)
+    hidden_out(third, 0, last_weight.at[0], 2, hidden, gain_pad, 3, fourth, None, NEW_FIRST, WHOLE)
 
     def finish(i, chunk, main, rest):
         main_in, rest_in = state_get(state, i, chunk)
         live = facts[1 + HALO + i][None, None, :]
         pack_dense(out, i, chunk, (main + main_in) * live, (rest + rest_in) * live)
 
-    residual_out(fourth, HALO, later_weight.at[2], 3, hidden, NEW_FIRST, LAST_SPLIT, finish)
+    residual_out(fourth, HALO, last_weight.at[1], 3, hidden, NEW_FIRST, LAST_SPLIT, finish)
 
 
 def fifth_kernel(
-    facts, swapped, crossed, later_weight, fourth_in, state, later, fourth, out, hidden, stage, sems
+    facts, swapped, crossed, last_weight, fourth_in, state, later, fourth, out, hidden, stage, sems
 ):
     keep = facts[0][None, None, :]
     copies = [pltpu.make_async_copy(later, out.at[pl.ds(HALO, HALO)], sems.at[0])]
@@ -397,7 +400,7 @@
             copies.append(pltpu.make_async_copy(stage.at[i, :, lanes], out.at[i, :, lanes], sem))
             copies[-1].start()
 
-    residual_out(fourth, 0, later_weight.at[2], 3, hidden, NEW_FIRST, END_SPLIT, finish)
+    residual_out(fourth, 0, last_weight.at[1], 3, hidden, NEW_FIRST, END_SPLIT, finish)
     for copy in copies:
         copy.wait()
 
@@ -476,7 +479,7 @@
             (block, gain_rows, weight0, weight_hbm),
             [vmem, vmem, vmem, hbm],
             carried,
-            (pieces, wire, weights(layers - 1)),
+            (pieces, wire, weights(1)),
             [hidden, dma],
             1,
         )
@@ -485,20 +488,20 @@
         return half(
             second_kernel,
             odd,
-            (known[1], halo, block, known[0], own, weight0, later_weight),
-            [vmem] * 7,
+            (known[1], halo, block, known[0], own, weight0, later_weight, weight_hbm),
+            [vmem] * 7 + [hbm],
             carried,
-            (pieces, pieces, state, wire),
-            [hidden],
+            (pieces, pieces, state, wire, weights(layers - 2)),
+            [hidden, dma],
             2,
         )
 
-    def step3(odd, known, halo, block, own, later_weight, carried):
+    def step3(odd, known, halo, block, own, later_weight, last_weight, carried):
         return half(
             third_kernel,
             odd,
-            (known[1], halo, block, known[0], own, later_weight),
-            [vmem] * 6,
+            (known[1], halo, block, known[0], own, later_weight, last_weight),
+            [vmem] * 7,
             carried,
             (pieces, pieces, state, wire),
             [hidden],
@@ -523,22 +526,24 @@
     crossed2, swapped2, even2, odd3 = exchange(
         odd2[3],
         lambda: step2(
-            False, known, crossed0, block, even1[1], weight0, later_weight, {0: odd2[0], 1: odd2[1], 2: odd2[2]}
+            False, known, crossed0, block, even1[1], weight0, later_weight, {n: odd2[n] for n in (0, 1, 2, 4)}
         ),
         3,
-        lambda even, _: step3(True, known, swapped1, block, odd2[3], later_weight, {0: even[1]}),
+        lambda even, _: step3(True, known, swapped1, block, odd2[3], later_weight, even[4], {0: even[1]}),
     )
-    state_late = even2[2]
+    state_late, last_weight = even2[2], even2[4]
 
     def last_steps(even, swapped):
         third = even[1]
         return call(
             fourth_kernel, [vmem] * 9, (pieces, pieces, dense_half), [hidden], 2, {7: 0}
-        )(known[1], swapped2, crossed2, known[0], odd3[3], even[3], later_weight, third, state_late)
+        )(known[1], swapped2, crossed2, known[0], odd3[3], even[3], last_weight, third, state_late)
 
     crossed3, swapped3, even3, (_, fourth, later) = exchange(
         odd3[3],
-        lambda: step3(False, known, crossed1, block, even2[3], later_weight, {0: odd3[0], 1: odd3[1], 2: odd3[2]}),
+        lambda: step3(
+            False, known, crossed1, block, even2[3], later_weight, last_weight, {0: odd3[0], 1: odd3[1], 2: odd3[2]}
+        ),
         3,
         last_steps,
     )
@@ -550,7 +555,7 @@
         1,
         {4: 0},
         (vmem, hbm),
-    )(known[1], swapped3, crossed3, later_weight, fourth, even3[2], later)
+    )(known[1], swapped3, crossed3, last_weight, fourth, even3[2], later)
     return out
 
 

time: 39.9 us -> 39.9 us (level)
  no operation moved by 1% of the time
where the time goes in v5:
time: 39.9 us; the launch traced here: 39.7 us
  Pallas kernels  23.9 us (60%)
  starting transfers between devices  15.4 us (39%)
    pallas_call x8, Pallas kernels, half(): call(kernel, specs + [vmem] * len(carried), outs, scratch, convs, aliases)  15.9 us
    ppermute x4, starting transfers between devices, exchange(): crossed = lax.ppermute(sent, 'tm', cross)  15.1 us
    pallas_call x1, Pallas kernels, last_steps(): call(fourth_kernel, [vmem] * 9, (pieces, pieces, dense_half), [hidden], 2...  4.82 us
    pallas_call x1, Pallas kernels, local(): call(fifth_kernel, [vmem] * 7, (pieces, dense), [hidden, VMEM(dense_half....  3.2 us
  transfers between devices with their start and end apart: 8, of which 0 were waited for; matrix products, arithmetic and copies ran while one was open for 0% of the time, Pallas kernels for 47%

profile of v5, /device:TPU:1, one launch (start us, length us, event | category | flops | bytes accessed | tf_op | source)
XLA Modules:
  0.0 39.7 jit_solution(14173289102761185353)
XLA Ops:
  0.0 2.1 %shard_map.55 = (bf16[6,26,16,640]{3,2,1,0:T(8,128)(2,1)S(1)}, bf16[2,16,4608]{2,1,0:T(8,128)(2,1)S(1)}, bf16[4,16,4608]{2,1,0:T(8,128)(2,1)S(1)}, bf16[1,27,192...) custom-call(bf16[4,16,4608]{2,1,0:T(8,128)(2,1)} %refs_0_.3, f32[4,192]{1,0:T(4,128)} %refs_1_.3, ...), custom_call_target="tpu_custom_call" | custom-call | bytes 4194304 | tf_op jit(solution)/shard_map/pallas_call | solution.py:459
  2.1 0.1 shard_map.56
  2.2 0.1 collective-permute-start.2
  2.3 4.5 %collective-permute-start.1 = (bf16[2,16,4608]{2,1,0:T(8,128)(2,1)S(1)}, bf16[2,16,4608]{2,1,0:T(8,128)(2,1)S(1)}, u32[]{:S(2)}, u32[]{:S(2)}) collective-permute-start(bf16[2,16,4608]{2,1,0:T(8,128)(2,1)S(1)} %get-tuple-element.53), channel_id=1, source_target_pairs={{1,2},{3,4},{5,6},{7,8},{9,10},{11,12},{13,14},{17,18},{19,20},{21... | collective-permute-start | bytes 884744 | tf_op jit(solution)/shard_map/ppermute | solution.py:462
  6.8 3.2 %shard_map.57 = (bf16[6,26,16,640]{3,2,1,0:T(8,128)(2,1)S(1)}, bf16[2,36,16,128]{3,2,1,0:T(8,128)(2,1)S(1)}, bf16[1,27,192,192]{3,2,1,0:T(8,128)(2,1)S(1)}) custom-call(bf16[4,16,4608]{2,1,0:T(8,128)(2,1)S(1)} %get-tuple-element.48.refs_0_.refs_2_, f32[4,2,128]{2,1,0:T(2,128)S(1)} %get-tuple-element.49.refs_1_.refs_3_.gain_pad, ...), custom_call_target="tpu_custom_call", output_to_operand_aliasing={{0}: (4, {})} | custom-call | flops 1528823808 | bytes 4194304 | tf_op jit(solution)/shard_map/pallas_call | solution.py:459
  10.1 0.1 collective-permute-start.3
  10.2 3.5 %collective-permute-start = (bf16[2,36,16,128]{3,2,1,0:T(8,128)(2,1)S(1)}, bf16[2,36,16,128]{3,2,1,0:T(8,128)(2,1)S(1)}, u32[]{:S(2)}, u32[]{:S(2)}) collective-permute-start(bf16[2,36,16,128]{3,2,1,0:T(8,128)(2,1)S(1)} %get-tuple-element.52.refs_4_), channel_id=1, source_target_pairs={{1,2},{3,4},{5,6},{7,8},{9,10},{11,12},{13,14},{17,18},{19,20},{21... | collective-permute-start | bytes 884744 | tf_op jit(solution)/shard_map/ppermute | solution.py:462
  13.7 0.0 collective-permute-done.2.refs_1_
  13.7 5.0 %shard_map.59 = (bf16[6,26,16,640]{3,2,1,0:T(8,128)(2,1)S(1)}, bf16[6,26,16,640]{3,2,1,0:T(8,128)(2,1)S(1)}, bf16[2,2,24,16,128]{4,3,2,1,0:T(8,128)(2,1)S(1)}, b...) custom-call(f32[8,128]{1,0:T(8,128)S(1)} %get-tuple-element.47.refs_0_.facts, ...), custom_call_target="tpu_custom_call", output_to_operand_aliasing={{0}: (8, {})} | custom-call | flops 3057647616 | bytes 4194304 | tf_op jit(solution)/shard_map/pallas_call | solution.py:459
  18.8 0.0 collective-permute-done.1.refs_1_
  18.8 0.2 shard_map.60
  19.0 0.1 collective-permute-start.6
  19.1 3.5 %collective-permute-start.7 = (bf16[2,36,16,128]{3,2,1,0:T(8,128)(2,1)S(1)}, bf16[2,36,16,128]{3,2,1,0:T(8,128)(2,1)S(1)}, u32[]{:S(2)}, u32[]{:S(2)}) collective-permute-start(bf16[2,36,16,128]{3,2,1,0:T(8,128)(2,1)S(1)} %get-tuple-element.66.refs_4_), channel_id=1, source_target_pairs={{1,2},{3,4},{5,6},{7,8},{9,10},{11,12},{13,14},{17,18},{19,20},{21... | collective-permute-start | bytes 884744 | tf_op jit(solution)/shard_map/ppermute | solution.py:462
  22.6 0.0 collective-permute-done.3.refs_1_
  22.6 5.0 %shard_map.61 = (bf16[6,26,16,640]{3,2,1,0:T(8,128)(2,1)S(1)}, bf16[6,26,16,640]{3,2,1,0:T(8,128)(2,1)S(1)}, bf16[2,2,24,16,128]{4,3,2,1,0:T(8,128)(2,1)S(1)}, bf16[2,36,16,128]{3,2,1,0:T(8,128)(2,1)S(1)}) custom-call(f32[8,128]{1,0:T(8,128)S(1)} %get-tuple-element.47.refs_0_.facts, ...), custom_call_target="tpu_custom_call", output_to_operand_aliasing={{0}: (7, {})} | custom-call | flops 3057647616 | bytes 4194304 | tf_op jit(solution)/shard_map/pallas_call | solution.py:459
  27.6 0.0 collective-permute-done.refs_1_
  27.6 0.2 shard_map.62
  27.9 0.1 collective-permute-start.4
  27.9 3.5 %collective-permute-start.5 = (bf16[2,36,16,128]{3,2,1,0:T(8,128)(2,1)S(1)}, bf16[2,36,16,128]{3,2,1,0:T(8,128)(2,1)S(1)}, u32[]{:S(2)}, u32[]{:S(2)}) collective-permute-start(bf16[2,36,16,128]{3,2,1,0:T(8,128)(2,1)S(1)} %get-tuple-element.72.own_odd), channel_id=1, source_target_pairs={{1,2},{3,4},{5,6},{7,8},{9,10},{11,12},{13,14},{17,18},{19,20},{21... | collective-permute-start | bytes 884744 | tf_op jit(solution)/shard_map/ppermute | solution.py:462
  31.5 0.0 collective-permute-done.6.swapped
  31.5 0.0 collective-permute-done.7.crossed
  31.5 4.8 %shard_map.63 = (bf16[6,26,16,640]{3,2,1,0:T(8,128)(2,1)S(1)}, bf16[6,26,16,640]{3,2,1,0:T(8,128)(2,1)S(1)}, bf16[2,16,4608]{2,1,0:T(8,128)(2,1)S(1)}) custom-call(f32[8,128]{1,0:T(8,128)S(1)} %get-tuple-element.47.refs_0_.facts, bf16[2,36,16,128]{3,2,1,0:T(8,128)(2,1)S(1)} %collective-permute-done.6.swapped, ...), custom_call_target="tpu_custom_call", output_to_operand_aliasing={{0}: (7, {})} | custom-call | flops 3057647616 | bytes 4194304 | tf_op jit(solution)/shard_map/pallas_call | solution.py:538
  36.3 0.0 collective-permute-done.4.swapped
  36.3 0.0 collective-permute-done.5.crossed
  36.3 3.2 %shard_map.64 = (bf16[6,26,16,640]{3,2,1,0:T(8,128)(2,1)S(1)}, bf16[4,16,4608]{2,1,0:T(8,128)(2,1)}) custom-call(f32[8,128]{1,0:T(8,128)S(1)} %get-tuple-element.47.refs_0_.facts, bf16[2,36,16,128]{3,2,1,0:T(8,128)(2,1)S(1)} %collective-permute-done.4.swapped, ...), custom_call_target="tpu_custom_call", output_to_operand_aliasing={{0}: (4, {})} | custom-call | flops 1528823808 | bytes 4194304 | tf_op jit(solution)/shard_map/pallas_call | solution.py:550
  (1 shorter events, 0.0 us)
Async XLA Ops:
  2.2 11.5 %collective-permute-start.2 = (bf16[2,16,4608]{2,1,0:T(8,128)(2,1)S(1)}, bf16[2,16,4608]{2,1,0:T(8,128)(2,1)S(1)}, u32[]{:S(2)}, u32[]{:S(2)}) collective-permute-start(bf16[2,16,4608]{2,1,0:T(8,128)(2,1)S(1)} %get-tuple-element.58), channel_id=1, source_target_pairs={{0,1},{1,0},{2,3},{3,2},{4,5},{5,4},{6,7},{7,6},{8,9},{9,8},{10,11... | collective-permute-start | bytes 884744 | tf_op jit(solution)/shard_map/ppermute | solution.py:464
  2.3 16.5 %collective-permute-start.1 = (bf16[2,16,4608]{2,1,0:T(8,128)(2,1)S(1)}, bf16[2,16,4608]{2,1,0:T(8,128)(2,1)S(1)}, u32[]{:S(2)}, u32[]{:S(2)}) collective-permute-start(bf16[2,16,4608]{2,1,0:T(8,128)(2,1)S(1)} %get-tuple-element.53), channel_id=1, source_target_pairs={{1,2},{3,4},{5,6},{7,8},{9,10},{11,12},{13,14},{17,18},{19,20},{21... | collective-permute-start | bytes 884744 | tf_op jit(solution)/shard_map/ppermute | solution.py:462
  10.1 12.5 %collective-permute-start.3 = (bf16[2,36,16,128]{3,2,1,0:T(8,128)(2,1)S(1)}, bf16[2,36,16,128]{3,2,1,0:T(8,128)(2,1)S(1)}, u32[]{:S(2)}, u32[]{:S(2)}) collective-permute-start(bf16[2,36,16,128]{3,2,1,0:T(8,128)(2,1)S(1)} %get-tuple-element.56.refs_4_), channel_id=1, source_target_pairs={{0,1},{1,0},{2,3},{3,2},{4,5},{5,4},{6,7},{7,6},{8,9},{9,8},{10,11... | collective-permute-start | bytes 884744 | tf_op jit(solution)/shard_map/ppermute | solution.py:464
  10.2 17.4 %collective-permute-start = (bf16[2,36,16,128]{3,2,1,0:T(8,128)(2,1)S(1)}, bf16[2,36,16,128]{3,2,1,0:T(8,128)(2,1)S(1)}, u32[]{:S(2)}, u32[]{:S(2)}) collective-permute-start(bf16[2,36,16,128]{3,2,1,0:T(8,128)(2,1)S(1)} %get-tuple-element.52.refs_4_), channel_id=1, source_target_pairs={{1,2},{3,4},{5,6},{7,8},{9,10},{11,12},{13,14},{17,18},{19,20},{21... | collective-permute-start | bytes 884744 | tf_op jit(solution)/shard_map/ppermute | solution.py:462
  19.0 12.5 %collective-permute-start.6 = (bf16[2,36,16,128]{3,2,1,0:T(8,128)(2,1)S(1)}, bf16[2,36,16,128]{3,2,1,0:T(8,128)(2,1)S(1)}, u32[]{:S(2)}, u32[]{:S(2)}) collective-permute-start(bf16[2,36,16,128]{3,2,1,0:T(8,128)(2,1)S(1)} %get-tuple-element.64.refs_4_), channel_id=1, source_target_pairs={{0,1},{1,0},{2,3},{3,2},{4,5},{5,4},{6,7},{7,6},{8,9},{9,8},{10,11... | collective-permute-start | bytes 884744 | tf_op jit(solution)/shard_map/ppermute | solution.py:464
  19.1 12.4 %collective-permute-start.7 = (bf16[2,36,16,128]{3,2,1,0:T(8,128)(2,1)S(1)}, bf16[2,36,16,128]{3,2,1,0:T(8,128)(2,1)S(1)}, u32[]{:S(2)}, u32[]{:S(2)}) collective-permute-start(bf16[2,36,16,128]{3,2,1,0:T(8,128)(2,1)S(1)} %get-tuple-element.66.refs_4_), channel_id=1, source_target_pairs={{1,2},{3,4},{5,6},{7,8},{9,10},{11,12},{13,14},{17,18},{19,20},{21... | collective-permute-start | bytes 884744 | tf_op jit(solution)/shard_map/ppermute | solution.py:462
  27.9 8.5 %collective-permute-start.4 = (bf16[2,36,16,128]{3,2,1,0:T(8,128)(2,1)S(1)}, bf16[2,36,16,128]{3,2,1,0:T(8,128)(2,1)S(1)}, u32[]{:S(2)}, u32[]{:S(2)}) collective-permute-start(bf16[2,36,16,128]{3,2,1,0:T(8,128)(2,1)S(1)} %get-tuple-element.71.own_even), channel_id=1, source_target_pairs={{0,1},{1,0},{2,3},{3,2},{4,5},{5,4},{6,7},{7,6},{8,9},{9,8},{10,11... | collective-permute-start | bytes 884744 | tf_op jit(solution)/shard_map/ppermute | solution.py:464
  27.9 8.4 %collective-permute-start.5 = (bf16[2,36,16,128]{3,2,1,0:T(8,128)(2,1)S(1)}, bf16[2,36,16,128]{3,2,1,0:T(8,128)(2,1)S(1)}, u32[]{:S(2)}, u32[]{:S(2)}) collective-permute-start(bf16[2,36,16,128]{3,2,1,0:T(8,128)(2,1)S(1)} %get-tuple-element.72.own_odd), channel_id=1, source_target_pairs={{1,2},{3,4},{5,6},{7,8},{9,10},{11,12},{13,14},{17,18},{19,20},{21... | collective-permute-start | bytes 884744 | tf_op jit(solution)/shard_map/ppermute | solution.py:462
